TPU v7x, 32 devices: a whole 2x2x4 slice. The times are simulated.
32 devices in a mesh: grp: 2 (over y), tile: 8 (over z, x), corner: 2 (over core).
Axes of the slice: x: 2, y: 2, z: 4, core: 2. Of those that a mesh axis runs over, the one named last changes fastest.
Arguments:
- mask_logits: float32 [768, 512], P(('grp', 'tile'), 'corner'), parts along dimension 0, may hold values from -1.5 to 1.5
- target: bfloat16 [768, 512], P(('grp', 'tile')), parts along dimension 0, may hold values from 0 to 1
- adam_first: float32 [768, 512], P(('grp', 'tile'), 'corner'), parts along dimension 0, may hold values from -1.5 to 1.5
- adam_second: float32 [768, 512], P(('grp', 'tile'), 'corner'), parts along dimension 0, may hold values from 0.05 to 0.2
- tile_counts: int32 [16, 4], P(('grp', 'tile')), parts along dimension 0, may hold values from 0 to 47
- kernels: float32 [2, 8, 2, 35, 35], P('corner'), may hold values from -0.15625 to 0.15625
- socs_weight: float32 [2, 8], P('corner'), may hold values from 0.03 to 0.3
- corner_dose: float32 [2], P('corner'), may hold values from 0.85 to 1.15
Outputs:
- out_logits: float32 [768, 512], P(('grp', 'tile'), 'corner'), parts along dimension 0
- out_first: float32 [768, 512], P(('grp', 'tile'), 'corner'), parts along dimension 0
- out_second: float32 [768, 512], P(('grp', 'tile'), 'corner'), parts along dimension 0
There are 2 independent parts, one for each index of `grp`. A program takes and returns all parts, laid end to end along the dimension named above; an argument that names none is the same for every part. Nothing has to cross between parts.
All inputs are finite; a program needn't handle non-finite values.
Results may differ from a plain program's by a relative error of at most 0.013.
Values may be sent and summed in bfloat16 or wider, within the bound.
No kernel may reach another device: no remote copies, remote signals or barrier semaphores. Data moves between devices by JAX's collectives and lax.ppermute only.
A program may use at most 64 MiB of HBM per device.

v0:
```python
import functools
import math

import jax
import jax.numpy as jnp
import numpy as np
from jax import lax
from jax.experimental import pallas as pl
from jax.experimental.pallas import tpu as pltpu
from jax.sharding import PartitionSpec as P


ITERS = 2

steep = 8.0
thresh = 0.5
loss_scale = 20.0
step_size = 0.05
beta_one = 0.9
beta_two = 0.999
adam_eps = 1e-08
prior_steps = 1000.0

LANES = 128
HALF_SPEC = 128
MIDDLE = 0.5
COL_LEN = 2 * HALF_SPEC
CHUNK = 16
GROUP = 2

BF = jnp.bfloat16
F32 = jnp.float32


def up_to(value, unit):
    return -(-value // unit) * unit


class Plan:
    def __init__(self, strip_rows, width, taps):
        reach = taps // 2
        self.strip_rows, self.width, self.taps, self.reach = strip_rows, width, taps, reach
        self.field_rows = strip_rows + 2 * reach
        self.field_pad = up_to(self.field_rows, 8)
        self.ext_rows = strip_rows + 4 * reach
        self.row_len = up_to(self.ext_rows, 128)
        self.taps_pad = up_to(taps, 8)
        self.col_tiles = width // LANES - 1
        self.starts = [LANES * t for t in range(self.col_tiles)]
        assert width % LANES == 0 and self.col_tiles >= 2
        assert LANES > 4 * reach
        edge = LANES // 2 - 8
        self.bounds = [0] + [s + edge for s in self.starts[1:]] + [width]

        omega = 2.0 * math.pi * (np.arange(HALF_SPEC) + 0.5) / COL_LEN
        phi = 2.0 * math.pi * np.arange(self.row_len) / self.row_len
        rows = np.arange(self.row_len)

        fwd = []
        for t, start in enumerate(self.starts):
            x = start + np.arange(COL_LEN)
            keep = np.ones(COL_LEN)
            if t == 0:
                keep = keep * (x < COL_LEN - reach)
            if t == self.col_tiles - 1:
                keep = keep * (x >= start + reach)
            angle = (x - start)[:, None] * omega[None, :]
            fwd.append(np.concatenate([np.cos(angle), -np.sin(angle)], 1) * keep[:, None])
        self.col_fwd = np.stack(fwd)
        edges = []
        for x in (np.arange(-reach, 0), COL_LEN + np.arange(reach)):
            angle = x[:, None] * omega[None, :]
            edge = -MIDDLE * np.concatenate([np.cos(angle), -np.sin(angle)], 1).sum(0)
            edges += split_table(edge)
        self.edges = np.stack(edges)
        self.col_adj = self.col_fwd.transpose(0, 2, 1)

        scale = 2.0 / (COL_LEN * self.row_len)
        angle = omega[:, None] * np.arange(COL_LEN)[None, :]
        self.col_inv = np.concatenate([np.cos(angle), -np.sin(angle)], 0) * scale
        self.col_inv_adj = self.col_inv.T

        angle = phi[:, None] * rows[None, :]
        live = (rows < self.ext_rows)[None, :]
        c, s = np.cos(angle) * live, np.sin(angle) * live
        mixed = np.arange(2 * self.row_len).reshape(2, -1, CHUNK).transpose(1, 0, 2).reshape(-1)
        self.row_fwd = np.block([[c, s], [-s, c]])[mixed]
        own = slice(2 * reach, 2 * reach + strip_rows)
        self.row_adj = np.block([[c[:, own].T, -s[:, own].T], [s[:, own].T, c[:, own].T]])[:, mixed]

        angle = (np.arange(self.field_pad) + reach)[:, None] * phi[None, :]
        live = (np.arange(self.field_pad) < self.field_rows)[:, None]
        c, s = np.cos(angle) * live, np.sin(angle) * live
        self.row_inv = np.block([[c, -s], [s, c]])[:, mixed]
        self.row_inv_adj = self.row_inv.T

        tap = np.arange(taps) - reach
        angle = tap[:, None] * omega[None, :]
        self.tap_cols = np.concatenate([np.cos(angle), -np.sin(angle)], 1)
        angle = phi[:, None] * tap[None, :]
        fill = ((0, 0), (0, self.taps_pad - taps))
        c, s = np.pad(np.cos(angle), fill), np.pad(np.sin(angle), fill)
        self.tap_rows = np.block([[c, s], [-s, c]])[mixed]


        rows_hi, rows_lo = split_table(self.tap_rows)
        cols_hi, cols_lo = split_table(self.tap_cols)
        parts = {
            "col_fwd": self.col_fwd.reshape(-1, COL_LEN),
            "col_adj": self.col_adj.reshape(-1, COL_LEN),
            "col_inv": self.col_inv,
            "col_inv_adj": self.col_inv_adj,
            "row_fwd": self.row_fwd,
            "row_adj": self.row_adj,
            "row_inv": self.row_inv,
            "row_inv_adj": self.row_inv_adj,
            "edges": self.edges,
        }
        tap_parts = {
            "tap_rows": np.concatenate([rows_hi, rows_lo, rows_hi], axis=1),
            "tap_hi": cols_hi,
            "tap_lo": cols_lo,
        }
        self.where = {}
        self.packed = self.pack(parts)
        self.tap_packed = self.pack(tap_parts)

    def pack(self, parts):
        packed, at = [], 0
        wide = max(part.shape[1] for part in parts.values())
        for name, part in parts.items():
            part = np.asarray(part, np.float32).astype(BF)
            self.where[name] = (at, part.shape[0], part.shape[1])
            fill = up_to(part.shape[0], CHUNK) - part.shape[0]
            packed.append(np.pad(part, ((0, fill), (0, wide - part.shape[1]))))
            at += part.shape[0] + fill
        return np.concatenate(packed, axis=0)

    def table(self, ref, name, block=None):
        at, rows, cols = self.where[name]
        if block is not None:
            at, rows = at + block * COL_LEN, COL_LEN
        return ref[at : at + rows, :cols]


@functools.lru_cache(maxsize=None)
def plan_of(strip_rows, width, taps):
    return Plan(strip_rows, width, taps)


def split_table(table):
    high = np.asarray(table, np.float32).astype(BF)
    low = (np.asarray(table, np.float64) - high.astype(np.float64)).astype(np.float32).astype(BF)
    return high, low


def dot(left, right):
    return lax.dot_general(left, right, (((1,), (0,)), ((), ())), preferred_element_type=F32)


def split(value):
    high = value.astype(BF)
    return high, (value - high.astype(F32)).astype(BF)


def fetch_body(
    logits_hbm,
    first_hbm,
    second_hbm,
    target_hbm,
    counts_hbm,
    mask_ref,
    state_ref,
    target_ref,
    counts_ref,
    flags_ref,
    counts_smem,
    sems,
):
    pairs = (
        (logits_hbm, state_ref.at[0]),
        (counts_hbm, counts_smem),
        (target_hbm, target_ref),
        (first_hbm, state_ref.at[1]),
        (second_hbm, state_ref.at[2]),
    )
    copies = [pltpu.make_async_copy(a, b, sems.at[i]) for i, (a, b) in enumerate(pairs)]
    for copy in copies:
        copy.start()
    place, corner = lax.axis_index("tile"), lax.axis_index("corner")
    facts = (corner == 0, place == 0, place == lax.axis_size("tile") - 1)
    for i, fact in enumerate(facts):
        flags_ref[i] = jnp.full((8, LANES), jnp.where(fact, 1.0, 0.0), F32)
    copies[0].wait()
    mask = (1.0 / (1.0 + jnp.exp(-state_ref[0]))).astype(BF)
    mask_ref[...] = (mask.astype(F32) - MIDDLE).astype(BF)
    for copy in copies[1:]:
        copy.wait()
    tiles = counts_smem.shape[1]
    wide = counts_ref.shape[1] // tiles
    for tile in range(tiles):
        value = counts_smem[0, tile].astype(F32)
        counts_ref[:, tile * wide : (tile + 1) * wide] = jnp.full((8, wide), value, F32)


def fetch(mask_logits, adam_first, adam_second, target, tile_counts):
    args = (mask_logits, adam_first, adam_second, target, tile_counts)
    shape = mask_logits.shape
    outs = (
        jax.ShapeDtypeStruct(shape, BF),
        jax.ShapeDtypeStruct((3,) + shape, F32),
        jax.ShapeDtypeStruct(target.shape, BF),
        jax.ShapeDtypeStruct((8, target.shape[1]), F32),
        jax.ShapeDtypeStruct((3, 8, LANES), F32),
    )
    return pl.pallas_call(
        fetch_body,
        out_shape=outs,
        in_specs=[pl.BlockSpec(memory_space=pltpu.HBM)] * len(args),
        out_specs=tuple(pl.BlockSpec(memory_space=pltpu.VMEM) for _ in outs),
        scratch_shapes=[
            pltpu.SMEM(tile_counts.shape, jnp.int32),
            pltpu.SemaphoreType.DMA((len(args),)),
        ],
        compiler_params=pltpu.CompilerParams(vmem_limit_bytes=4 * 1024 * 1024),
        name="fetch",
    )(*(pltpu.with_memory_space_constraint(value, pltpu.HBM) for value in args))


def spectra_body(
    plan,
    weight_hbm,
    kern_hbm,
    table_hbm,
    out_ref,
    level_ref,
    weight_ref,
    kern_ref,
    table_ref,
    sems,
):
    copies = [
        pltpu.make_async_copy(kern_hbm, kern_ref, sems.at[0]),
        pltpu.make_async_copy(table_hbm, table_ref, sems.at[1]),
        pltpu.make_async_copy(weight_hbm, weight_ref, sems.at[2]),
    ]
    for copy in copies:
        copy.start()
    for copy in copies:
        copy.wait()
    count = out_ref.shape[0]
    pad = plan.taps_pad - plan.taps
    stack, sums = [], []
    for k in range(count):
        taps = kern_ref[k // 2, :, k % 2, :]
        sums.append(jnp.sum(taps, axis=0, keepdims=True))
        stack.append(jnp.concatenate([taps, jnp.zeros((pad, plan.taps), F32)], axis=0))
    hi, lo = split(jnp.concatenate(stack, axis=0))
    sums = MIDDLE * jnp.sum(jnp.concatenate(sums, axis=0), axis=1, keepdims=True)
    sums = jnp.broadcast_to(sums, (count, COL_LEN))
    cols_hi, cols_lo = plan.table(table_ref, "tap_hi"), plan.table(table_ref, "tap_lo")
    half = dot(hi, cols_hi) + dot(lo, cols_hi) + dot(hi, cols_lo)
    for k in range(0, count, 2):
        both = []
        for part in (k, k + 1):
            one = half[part * plan.taps_pad : (part + 1) * plan.taps_pad]
            both.append(jnp.concatenate([one[:, :HALF_SPEC], one[:, HALF_SPEC:]], axis=0))
        hi, lo = split(jnp.concatenate(both, axis=1))
        spec = dot(plan.table(table_ref, "tap_rows"), jnp.concatenate([hi, hi, lo], axis=0))
        root_wide = jnp.sqrt(jnp.full((8, COL_LEN), weight_ref[0, k // 2], F32))
        root = root_wide[:1, :HALF_SPEC]
        for part in (k, k + 1):
            level_ref[part] = root_wide * sums[part : part + 1]
        out_ref[k] = spec[:, :HALF_SPEC] * root
        out_ref[k + 1] = spec[:, HALF_SPEC:] * root


def kernel_spectra(plan, kernels, socs_weight):
    count = kernels.shape[1] * kernels.shape[2]
    taps = kernels[0].transpose(0, 2, 1, 3)
    tables = plan.tap_packed
    hbm = pl.BlockSpec(memory_space=pltpu.HBM)
    return pl.pallas_call(
        functools.partial(spectra_body, plan),
        out_shape=(
            jax.ShapeDtypeStruct((count, 2 * plan.row_len, HALF_SPEC), F32),
            jax.ShapeDtypeStruct((count, 8, COL_LEN), F32),
        ),
        in_specs=[hbm] * 3,
        out_specs=(pl.BlockSpec(memory_space=pltpu.VMEM), pl.BlockSpec(memory_space=pltpu.VMEM)),
        scratch_shapes=[
            pltpu.SMEM(socs_weight.shape, F32),
            pltpu.VMEM(taps.shape, F32),
            pltpu.VMEM(tables.shape, BF),
            pltpu.SemaphoreType.DMA((3,)),
        ],
        compiler_params=pltpu.CompilerParams(vmem_limit_bytes=4 * 1024 * 1024),
        name="spectra",
    )(
        *(
            pltpu.with_memory_space_constraint(value, pltpu.HBM)
            for value in (socs_weight, taps, jnp.asarray(tables))
        ),
    )


def gradient_body(
    plan,
    dose_ref,
    mask_ref,
    target_ref,
    weight_ref,
    spec_ref,
    level_ref,
    table_ref,
    out_ref,
    s_ref,
    field_ref,
    light_ref,
    acc_ref,
    hold_ref,
    back_ref,
):
    tiles = plan.col_tiles
    rows = plan.row_len
    fr = plan.field_pad
    g = HALF_SPEC
    count = spec_ref.shape[0]

    along = []
    edges = plan.table(table_ref, "edges").astype(F32)
    for t in range(tiles):
        window = mask_ref[:, plan.starts[t] : plan.starts[t] + COL_LEN]
        a = dot(window, plan.table(table_ref, "col_fwd", t))
        if t == 0:
            a = a + (edges[0:1] + edges[1:2])
        if t == tiles - 1:
            a = a + (edges[2:3] + edges[3:4])
        along.append(jnp.concatenate([a[:, :g], a[:, g:]], axis=0).astype(BF))
    s_ref[...] = dot(plan.table(table_ref, "row_fwd"), jnp.concatenate(along, axis=1))
    light_ref[...] = jnp.zeros_like(light_ref)
    acc_ref[...] = jnp.zeros_like(acc_ref)
    chunks = [(at, at + CHUNK, at + 2 * CHUNK) for at in range(0, 2 * rows, 2 * CHUNK)]

    groups = count // GROUP

    def multiply(group):
        passed = []
        for t in range(tiles):
            lane = slice(t * g, t * g + g)
            prods = [[] for _ in range(GROUP)]
            for a, b, c in chunks:
                s_re, s_im = s_ref[a:b, lane], s_ref[b:c, lane]
                for part in range(GROUP):
                    k = GROUP * group + part
                    k_re, k_im = spec_ref[k, a:b], spec_ref[k, b:c]
                    prods[part].append((s_re * k_re - s_im * k_im).astype(BF))
                    prods[part].append((s_re * k_im + s_im * k_re).astype(BF))
            block = jnp.concatenate([jnp.concatenate(p, axis=0) for p in prods], axis=1)
            passed.append(dot(plan.table(table_ref, "row_inv"), block))
        stack = []
        for t in range(tiles):
            for part in range(GROUP):
                lane = slice(part * g, part * g + g)
                stack.append(jnp.concatenate([passed[t][:fr, lane], passed[t][fr:, lane]], axis=1))
        hold_ref[group % 2] = jnp.concatenate(stack, axis=0).astype(BF)

    def image(group):
        field = dot(hold_ref[group % 2], plan.table(table_ref, "col_inv"))
        for t in range(tiles):
            total = light_ref[t]
            for part in range(GROUP):
                at = (GROUP * t + part) * fr
                one = field[at : at + fr] + level_ref[GROUP * group + part, :1]
                field_ref[group, at : at + fr] = one
                total = total + one * one
            light_ref[t] = total

    def forward(group, carry):
        image(group)
        multiply(group + 1)
        return carry

    multiply(0)
    lax.fori_loop(0, groups - 1, forward, 0)
    image(groups - 1)

    dose = dose_ref[:1, :1]
    row = lax.broadcasted_iota(jnp.int32, (fr, COL_LEN), 0)
    col = lax.broadcasted_iota(jnp.int32, (fr, COL_LEN), 1)
    reach, strip = plan.reach, plan.strip_rows
    for t in range(tiles):
        lane = slice(plan.starts[t], plan.starts[t] + COL_LEN)
        resist = 1.0 / (1.0 + jnp.exp(-steep * (dose * light_ref[t] - thresh)))
        missed = resist - target_ref[:, lane].astype(F32)
        above, here, below = (weight_ref[i : i + 1, lane] for i in range(3))
        weight = jnp.where(row < reach, above, jnp.where(row < reach + strip, here, below))
        low, high = plan.bounds[t] - plan.starts[t], plan.bounds[t + 1] - plan.starts[t]
        kept = (row < plan.field_rows) & (col >= low) & (col < high)
        weight = jnp.where(kept, weight, 0.0)
        factor = 4.0 * loss_scale * steep * dose
        light_ref[t] = factor * weight * missed * resist * (1.0 - resist)

    def image_back(group):
        stack = []
        for t in range(tiles):
            for part in range(GROUP):
                at = (GROUP * t + part) * fr
                stack.append(light_ref[t] * field_ref[group, at : at + fr])
        inner = dot(jnp.concatenate(stack, axis=0).astype(BF), plan.table(table_ref, "col_inv_adj"))
        for t in range(tiles):
            block = []
            for part in range(GROUP):
                at = (GROUP * t + part) * fr
                d = inner[at : at + fr]
                block.append(jnp.concatenate([d[:, :g], d[:, g:]], axis=0))
            back_ref[group % 2, t] = jnp.concatenate(block, axis=1).astype(BF)

    def multiply_back(group):
        for t in range(tiles):
            lane = slice(t * g, t * g + g)
            d_prod = dot(plan.table(table_ref, "row_inv_adj"), back_ref[group % 2, t])
            for a, b, c in chunks:
                sum_re, sum_im = acc_ref[a:b, lane], acc_ref[b:c, lane]
                for part in range(GROUP):
                    k = GROUP * group + part
                    k_re, k_im = spec_ref[k, a:b], spec_ref[k, b:c]
                    at = slice(part * g, part * g + g)
                    d_re, d_im = d_prod[a:b, at], d_prod[b:c, at]
                    sum_re = sum_re + (d_re * k_re + d_im * k_im)
                    sum_im = sum_im + (d_im * k_re - d_re * k_im)
                acc_ref[a:b, lane] = sum_re
                acc_ref[b:c, lane] = sum_im

    def backward(group, carry):
        multiply_back(group)
        image_back(group + 1)
        return carry

    image_back(0)
    lax.fori_loop(0, groups - 1, backward, 0)
    multiply_back(groups - 1)

    d_along = dot(plan.table(table_ref, "row_adj"), acc_ref[...].astype(BF))
    parts = []
    for t in range(tiles):
        lane = slice(t * g, t * g + g)
        both = jnp.concatenate([d_along[:strip, lane], d_along[strip:, lane]], axis=1).astype(BF)
        parts.append(dot(both, plan.table(table_ref, "col_adj", t)))
    blocks = []
    for b in range(plan.width // LANES):
        terms = []
        for t in range(tiles):
            at = b * LANES - plan.starts[t]
            if 0 <= at < COL_LEN:
                terms.append(parts[t][:, at : at + LANES])
        blocks.append(functools.reduce(lambda x, y: x + y, terms))
    out_ref[...] = jnp.concatenate(blocks, axis=1)


def strip_gradient(plan, mask_ext, target_ext, weights, spec, dose, tables):
    vmem = pl.BlockSpec(memory_space=pltpu.VMEM)
    count = spec[0].shape[0]
    spectrum = (2 * plan.row_len, plan.col_tiles * HALF_SPEC)
    image = (plan.col_tiles, plan.field_pad, COL_LEN)
    return pl.pallas_call(
        functools.partial(gradient_body, plan),
        out_shape=jax.ShapeDtypeStruct((plan.strip_rows, plan.width), F32),
        in_specs=[vmem] * 7,
        out_specs=vmem,
        scratch_shapes=[
            pltpu.VMEM(spectrum, F32),
            pltpu.VMEM((count // GROUP, GROUP * plan.col_tiles * plan.field_pad, COL_LEN), F32),
            pltpu.VMEM(image, F32),
            pltpu.VMEM(spectrum, F32),
            pltpu.VMEM((2, GROUP * plan.col_tiles * plan.field_pad, COL_LEN), BF),
            pltpu.VMEM((2, plan.col_tiles, 2 * plan.field_pad, GROUP * HALF_SPEC), BF),
        ],
        compiler_params=pltpu.CompilerParams(vmem_limit_bytes=12 * 1024 * 1024),
        name="gradient",
    )(dose, mask_ext, target_ext, weights, *spec, tables)


def other_corner(value):
    return lax.ppermute(value, "corner", [(0, 1), (1, 0)])


def neighbours(flags, top, bottom, blank):
    strips = lax.axis_size("tile")
    first_corner, highest, lowest = flags
    cycle = [(2 * i, 2 * i + 2) for i in range(strips - 1)] + [(2 * strips - 2, 2 * strips - 1)]
    cycle += [(2 * i + 1, 2 * i - 1) for i in range(1, strips)] + [(1, 0)]
    message = jnp.where(first_corner, bottom, top)
    got = lax.ppermute(message, ("tile", "corner"), cycle)
    shared = other_corner(got)
    above = jnp.where(highest, blank, jnp.where(first_corner, got, shared))
    below = jnp.where(lowest, blank, jnp.where(first_corner, shared, got))
    return above, below


def per_device(
    mask_logits, target, adam_first, adam_second, tile_counts, kernels, socs_weight, corner_dose
):
    strip_rows, half_width = mask_logits.shape
    width = target.shape[1]
    plan = plan_of(strip_rows, width, kernels.shape[-1])
    reach = plan.reach
    halo = 2 * reach

    def whole(own, other):
        left = jnp.where(first_corner, own, other)
        right = jnp.where(first_corner, other, own)
        return jnp.concatenate([left, right], axis=-1)

    def own_half(value):
        return jnp.where(first_corner, value[..., :half_width], value[..., half_width:])

    def extended(above_rows, own, below_rows, total):
        have = above_rows.shape[0] + own.shape[0] + below_rows.shape[0]
        blank = jnp.zeros((total - have, own.shape[1]), own.dtype)
        return jnp.concatenate([above_rows, own, below_rows, blank], axis=0)

    tables = jnp.asarray(plan.packed)

    mask_half, state, target, counts, facts = fetch(
        mask_logits, adam_first, adam_second, target, tile_counts
    )
    flags = [facts[i, :1, :1] > 0.5 for i in range(3)]
    first_corner = flags[0]
    dose = jnp.broadcast_to(corner_dose[None], (8, LANES))
    counts = counts[:1]
    counts_bf = counts.astype(BF)
    other_half = other_corner(mask_half)
    mask_bf = whole(mask_half, other_half)
    above, below = neighbours(
        flags,
        jnp.concatenate([mask_bf[:halo], target[:reach], counts_bf], axis=0),
        jnp.concatenate([mask_bf[-halo:], target[-reach:], counts_bf], axis=0),
        jnp.where(jnp.arange(halo + reach + 1)[:, None] < halo, -MIDDLE, 0.0).astype(BF),
    )
    spec = kernel_spectra(plan, kernels, socs_weight)
    target_ext = extended(
        above[halo : halo + reach], target, below[halo : halo + reach], plan.field_pad
    )
    near = jnp.concatenate(
        [above[halo + reach :].astype(F32), counts, below[halo + reach :].astype(F32)]
    )
    near = jnp.pad(near, ((0, 5), (0, 0)))
    weights = near / (near + 4.0)
    above, below = above[:halo], below[:halo]
    mask_ext = extended(above, mask_bf, below, plan.row_len)
    state = whole(state, other_corner(state))
    partial = strip_gradient(plan, mask_ext, target_ext, weights, spec, dose, tables)

    logits, first, second = state[0], state[1], state[2]
    opacity = jax.nn.sigmoid(logits)
    for iteration in range(ITERS):
        if iteration:
            opacity = jax.nn.sigmoid(logits)
            mask_bf = (lax.reduce_precision(opacity, 8, 7) - MIDDLE).astype(BF)
            blank = jnp.full((halo, 1), -MIDDLE, BF)
            above, below = neighbours(flags, mask_bf[:halo], mask_bf[-halo:], blank)
            mask_ext = extended(above, mask_bf, below, plan.row_len)
            partial = strip_gradient(plan, mask_ext, target_ext, weights, spec, dose, tables)
        if iteration < ITERS - 1:
            summed = partial + other_corner(partial.astype(BF)).astype(F32)
        else:
            mine = own_half(partial)
            theirs = jnp.where(first_corner, partial[:, half_width:], partial[:, :half_width])
            summed = mine + other_corner(theirs.astype(BF)).astype(F32)
            opacity, logits = own_half(opacity), own_half(logits)
            first, second = own_half(first), own_half(second)
        gradient = summed * opacity * (1.0 - opacity)
        count_now = prior_steps + iteration + 1.0
        first = beta_one * first + (1.0 - beta_one) * gradient
        second = beta_two * second + (1.0 - beta_two) * gradient * gradient
        first_hat = first / (1.0 - beta_one**count_now)
        second_hat = second / (1.0 - beta_two**count_now)
        logits = logits - step_size * first_hat / (jnp.sqrt(second_hat) + adam_eps)
    return (logits, first, second)


def solution(mesh):
    return jax.shard_map(
        per_device,
        mesh=mesh,
        in_specs=(
            P(("grp", "tile"), "corner"),
            P(("grp", "tile"), None),
            P(("grp", "tile"), "corner"),
            P(("grp", "tile"), "corner"),
            P(("grp", "tile"), None),
            P("corner", None, None, None, None),
            P("corner", None),
            P("corner"),
        ),
        out_specs=(
            P(("grp", "tile"), "corner"),
            P(("grp", "tile"), "corner"),
            P(("grp", "tile"), "corner"),
        ),
        check_vma=False,
    )
```

profile of v0, /device:TPU:21, one launch (start us, length us, event | category | flops | bytes accessed | tf_op | source)
XLA Modules:
  0.0 36.3 jit_solution(10388063858748134020)
XLA Ops:
  0.6 1.0 %fetch.1 = (bf16[48,256]{1,0:T(8,128)(2,1)S(1)}, f32[3,48,256]{2,1,0:T(8,128)S(1)}, bf16[48,512]{1,0:T(8,128)(2,1)S(1)}, f32[8,512]{1,0:T(8,128)S(1)}, f32[3,8,128]{2,1,0:T(8,128)S(1)}) custom-call(f32[48,256]{1,0:T(8,128)} %logits_hbm.1, f32[48,256]{1,0:T(8,128)} %first_hbm.1, f32[48,256]{1,0:T(8,128)} %second_hbm.1, bf16[48,512]{1,0:T(8,128)(2,1)} %target_hbm.1, ...), custom_call_target="tpu_custom_call" | custom-call | tf_op jit(solution)/shard_map/fetch/pallas_call | solution.py:216
  1.7 0.7 %collective-permute-start.1 = (bf16[48,256]{1,0:T(8,128)(2,1)S(1)}, bf16[48,256]{1,0:T(8,128)(2,1)S(1)}, u32[]{:S(2)}, u32[]{:S(2)}) collective-permute-start(bf16[48,256]{1,0:T(8,128)(2,1)S(1)} %get-tuple-element.12), channel_id=1, source_target_pairs={{0,1},{1,0},{2,3},{3,2},{4,5},{5,4},{6,7},{7,6},{8,9},{9,8},{10,11... | collective-permute-start | bytes 73736 | tf_op jit(solution)/shard_map/ppermute | solution.py:485
  2.4 0.5 %fusion.26 = (f32[1,1,1]{2,1,0:T(1,128)}, f32[1,1,1]{2,1,0:T(1,128)}, f32[1,1,1]{2,1,0:T(1,128)}) fusion(f32[3,8,128]{2,1,0:T(8,128)S(1)} %get-tuple-element.10), kind=kLoop, calls=%fused_computation.64 | loop fusion | bytes 24 | tf_op jit(solution)/shard_map/slice | solution.py:528
  3.7 1.2 %collective-permute-start.2 = (bf16[52,512]{1,0:T(8,128)(2,1)S(1)}, bf16[52,512]{1,0:T(8,128)(2,1)S(1)}, u32[]{:S(2)}, u32[]{:S(2)}) collective-permute-start(bf16[52,512]{1,0:T(8,128)(2,1)S(1)} %fusion.11), channel_id=1, source_target_pairs={{0,2},{2,4},{4,6},{6,8},{8,10},{10,12},{12,14},{14,15},{3,1},{5,3}... | collective-permute-start | bytes 159752 | tf_op jit(solution)/shard_map/ppermute | solution.py:494
  4.9 0.4 %collective-permute-start = (f32[3,48,256]{2,1,0:T(8,128)S(1)}, f32[3,48,256]{2,1,0:T(8,128)S(1)}, u32[]{:S(2)}, u32[]{:S(2)}) collective-permute-start(f32[3,48,256]{2,1,0:T(8,128)S(1)} %get-tuple-element.11), channel_id=1, source_target_pairs={{0,1},{1,0},{2,3},{3,2},{4,5},{5,4},{6,7},{7,6},{8,9},{9,8},{10,11... | collective-permute-start | bytes 442376 | tf_op jit(solution)/shard_map/ppermute | solution.py:485
  5.3 1.5 %collective-permute-done.2 = bf16[52,512]{1,0:T(8,128)(2,1)S(1)} collective-permute-done((bf16[52,512]{1,0:T(8,128)(2,1)S(1)}, bf16[52,512]{1,0:T(8,128)(2,1)S(1)}, u32[]{:S(2)}, u32[]{:S(2)}) %collective-permute-start.2) | collective-permute-done | bytes 53280 | tf_op jit(solution)/shard_map/ppermute | solution.py:494
  6.8 2.1 %collective-permute-start.3 = (bf16[52,512]{1,0:T(8,128)(2,1)S(1)}, bf16[52,512]{1,0:T(8,128)(2,1)S(1)}, u32[]{:S(2)}, u32[]{:S(2)}) collective-permute-start(bf16[52,512]{1,0:T(8,128)(2,1)S(1)} %collective-permute-done.2), channel_id=1, source_target_pairs={{0,1},{1,0},{2,3},{3,2},{4,5},{5,4},{6,7},{7,6},{8,9},{9,8},{10,11... | collective-permute-start | bytes 159752 | tf_op jit(solution)/shard_map/ppermute | solution.py:485
  9.6 0.1 pad.20.clone
  11.0 2.2 %spectra.1 = (f32[16,256,128]{2,1,0:T(8,128)S(1)}, f32[16,8,256]{2,1,0:T(8,128)S(1)}) custom-call(f32[1,8]{1,0:T(1,128)} %weight_hbm.1, f32[8,35,2,35]{3,2,1,0:T(2,128)} %bitcast.25, bf16[352,256]{1,0:T(8,128)(2,1)} %constant.16.clone.table_hbm), custom_call_target="tpu_custom_call" | custom-call | tf_op jit(solution)/shard_map/spectra/pallas_call | solution.py:283
  13.2 0.1 select_select_fusion.1
  13.4 0.1 maximum_maximum_fusion.2.target_ref
  13.5 0.1 maximum_maximum_fusion.mask_ref
  13.6 6.6 %gradient.2 = f32[48,512]{1,0:T(8,128)S(1)} custom-call(f32[8,128]{1,0:T(8,128)S(1)} %broadcast_in_dim.152.dose_ref, bf16[128,512]{1,0:T(8,128)(2,1)S(1)} %maximum_maximum_fusion.mask_ref, bf16[88,512]{1,0:T(8,128)(2,1)S(1)} %maximum_maximum_fusion.2.target_ref, f32[8,512]{1,0:T(8,128)S(1)} %add_divide_fusion.1.weight_ref, ...), custom_call_target="tpu_custom_call" | custom-call | tf_op jit(solution)/shard_map/gradient/pallas_call | solution.py:466
  20.3 1.2 %collective-permute-done.4 = bf16[48,512]{1,0:T(8,128)(2,1)S(1)} collective-permute-done((bf16[48,512]{1,0:T(8,128)(2,1)S(1)}, bf16[48,512]{1,0:T(8,128)(2,1)S(1)}, u32[]{:S(2)}, u32[]{:S(2)}) %collective-permute-start.4) | collective-permute-done | bytes 49184 | tf_op jit(solution)/shard_map/ppermute | solution.py:485
  21.5 0.1 add_convert_fusion
  21.7 0.9 %collective-permute-start.5 = (bf16[34,512]{1,0:T(8,128)(2,1)S(1)}, bf16[34,512]{1,0:T(8,128)(2,1)S(1)}, u32[]{:S(2)}, u32[]{:S(2)}) collective-permute-start(bf16[34,512]{1,0:T(8,128)(2,1)S(1)} %slice_select_fusion.4), channel_id=1, source_target_pairs={{0,2},{2,4},{4,6},{6,8},{8,10},{10,12},{12,14},{14,15},{3,1},{5,3}... | collective-permute-start | bytes 104456 | tf_op jit(solution)/shard_map/ppermute | solution.py:494
  22.6 2.0 %collective-permute-done.5 = bf16[34,512]{1,0:T(8,128)(2,1)S(1)} collective-permute-done((bf16[34,512]{1,0:T(8,128)(2,1)S(1)}, bf16[34,512]{1,0:T(8,128)(2,1)S(1)}, u32[]{:S(2)}, u32[]{:S(2)}) %collective-permute-start.5) | collective-permute-done | bytes 34848 | tf_op jit(solution)/shard_map/ppermute | solution.py:494
  24.6 2.2 %collective-permute-start.6 = (bf16[34,512]{1,0:T(8,128)(2,1)S(1)}, bf16[34,512]{1,0:T(8,128)(2,1)S(1)}, u32[]{:S(2)}, u32[]{:S(2)}) collective-permute-start(bf16[34,512]{1,0:T(8,128)(2,1)S(1)} %collective-permute-done.5), channel_id=1, source_target_pairs={{0,1},{1,0},{2,3},{3,2},{4,5},{5,4},{6,7},{7,6},{8,9},{9,8},{10,11... | collective-permute-start | bytes 104456 | tf_op jit(solution)/shard_map/ppermute | solution.py:485
  26.8 0.9 %collective-permute-done.6 = bf16[34,512]{1,0:T(8,128)(2,1)S(1)} collective-permute-done((bf16[34,512]{1,0:T(8,128)(2,1)S(1)}, bf16[34,512]{1,0:T(8,128)(2,1)S(1)}, u32[]{:S(2)}, u32[]{:S(2)}) %collective-permute-start.6) | collective-permute-done | bytes 34848 | tf_op jit(solution)/shard_map/ppermute | solution.py:485
  27.7 0.1 maximum_maximum_fusion.1.mask_ref
  27.8 6.6 %gradient.3 = f32[48,512]{1,0:T(8,128)S(1)} custom-call(f32[8,128]{1,0:T(8,128)S(1)} %broadcast_in_dim.152.dose_ref, bf16[128,512]{1,0:T(8,128)(2,1)S(1)} %maximum_maximum_fusion.1.mask_ref, bf16[88,512]{1,0:T(8,128)(2,1)S(1)} %maximum_maximum_fusion.2.target_ref, f32[8,512]{1,0:T(8,128)S(1)} %add_divide_fusion.1.weight_ref, ...), custom_call_target="tpu_custom_call" | custom-call | tf_op jit(solution)/shard_map/gradient/pallas_call | solution.py:466
  34.4 0.4 %collective-permute-start.7 = (bf16[48,256]{1,0:T(8,128)(2,1)S(1)}, bf16[48,256]{1,0:T(8,128)(2,1)S(1)}, u32[]{:S(2)}, u32[]{:S(2)}) collective-permute-start(bf16[48,256]{1,0:T(8,128)(2,1)S(1)} %select_convert_fusion), channel_id=1, source_target_pairs={{0,1},{1,0},{2,3},{3,2},{4,5},{5,4},{6,7},{7,6},{8,9},{9,8},{10,11... | collective-permute-start | bytes 73736 | tf_op jit(solution)/shard_map/ppermute | solution.py:485
  34.8 0.8 %collective-permute-done.7 = bf16[48,256]{1,0:T(8,128)(2,1)S(1)} collective-permute-done((bf16[48,256]{1,0:T(8,128)(2,1)S(1)}, bf16[48,256]{1,0:T(8,128)(2,1)S(1)}, u32[]{:S(2)}, u32[]{:S(2)}) %collective-permute-start.7) | collective-permute-done | bytes 24608 | tf_op jit(solution)/shard_map/ppermute | solution.py:485
  35.6 0.7 %fusion.18 = (f32[48,256]{1,0:T(8,128)}, f32[48,256]{1,0:T(8,128)}, f32[48,256]{1,0:T(8,128)}) fusion(f32[48,512]{1,0:T(8,128)S(1)} %get-tuple-element.22, pred[]{:T(512)} %bitcast, f32[48,512]{1,0:T(8,128)S(1)} %get-tuple-element.23, f32[48,512]{1,0:T(8,128)S(1)} %get-tuple-element.24, f32[48,512]{1,0:T(8,128)S(1)} %get-tuple-element.21, ...), kind=kLoop, calls=%fused_computation.43 | loop fusion | flops 270336 | bytes 663553 | tf_op jit(solution)/shard_map/sub | solution.py:579
  (28 shorter events, 0.4 us)
Async XLA Ops:
  0.6 13.0 %copy-start = (bf16[2848,256]{1,0:T(8,128)(2,1)S(1)}, bf16[2848,256]{1,0:T(8,128)(2,1)}, u32[]{:S(2)}) copy-start(bf16[2848,256]{1,0:T(8,128)(2,1)} %constant.15.clone.table_ref) | copy-start | bytes 4374532
  1.7 1.9 %collective-permute-start.1 = (bf16[48,256]{1,0:T(8,128)(2,1)S(1)}, bf16[48,256]{1,0:T(8,128)(2,1)S(1)}, u32[]{:S(2)}, u32[]{:S(2)}) collective-permute-start(bf16[48,256]{1,0:T(8,128)(2,1)S(1)} %get-tuple-element.12), channel_id=1, source_target_pairs={{0,1},{1,0},{2,3},{3,2},{4,5},{5,4},{6,7},{7,6},{8,9},{9,8},{10,11... | collective-permute-start | bytes 73736 | tf_op jit(solution)/shard_map/ppermute | solution.py:485
  3.7 3.1 %collective-permute-start.2 = (bf16[52,512]{1,0:T(8,128)(2,1)S(1)}, bf16[52,512]{1,0:T(8,128)(2,1)S(1)}, u32[]{:S(2)}, u32[]{:S(2)}) collective-permute-start(bf16[52,512]{1,0:T(8,128)(2,1)S(1)} %fusion.11), channel_id=1, source_target_pairs={{0,2},{2,4},{4,6},{6,8},{8,10},{10,12},{12,14},{14,15},{3,1},{5,3}... | collective-permute-start | bytes 159752 | tf_op jit(solution)/shard_map/ppermute | solution.py:494
  4.9 15.4 %collective-permute-start = (f32[3,48,256]{2,1,0:T(8,128)S(1)}, f32[3,48,256]{2,1,0:T(8,128)S(1)}, u32[]{:S(2)}, u32[]{:S(2)}) collective-permute-start(f32[3,48,256]{2,1,0:T(8,128)S(1)} %get-tuple-element.11), channel_id=1, source_target_pairs={{0,1},{1,0},{2,3},{3,2},{4,5},{5,4},{6,7},{7,6},{8,9},{9,8},{10,11... | collective-permute-start | bytes 442376 | tf_op jit(solution)/shard_map/ppermute | solution.py:485
  6.8 6.4 %collective-permute-start.3 = (bf16[52,512]{1,0:T(8,128)(2,1)S(1)}, bf16[52,512]{1,0:T(8,128)(2,1)S(1)}, u32[]{:S(2)}, u32[]{:S(2)}) collective-permute-start(bf16[52,512]{1,0:T(8,128)(2,1)S(1)} %collective-permute-done.2), channel_id=1, source_target_pairs={{0,1},{1,0},{2,3},{3,2},{4,5},{5,4},{6,7},{7,6},{8,9},{9,8},{10,11... | collective-permute-start | bytes 159752 | tf_op jit(solution)/shard_map/ppermute | solution.py:485
  20.2 1.3 %collective-permute-start.4 = (bf16[48,512]{1,0:T(8,128)(2,1)S(1)}, bf16[48,512]{1,0:T(8,128)(2,1)S(1)}, u32[]{:S(2)}, u32[]{:S(2)}) collective-permute-start(bf16[48,512]{1,0:T(8,128)(2,1)S(1)} %convert_element_type.40), channel_id=1, source_target_pairs={{0,1},{1,0},{2,3},{3,2},{4,5},{5,4},{6,7},{7,6},{8,9},{9,8},{10,11... | collective-permute-start | bytes 147464 | tf_op jit(solution)/shard_map/ppermute | solution.py:485
  21.7 2.9 %collective-permute-start.5 = (bf16[34,512]{1,0:T(8,128)(2,1)S(1)}, bf16[34,512]{1,0:T(8,128)(2,1)S(1)}, u32[]{:S(2)}, u32[]{:S(2)}) collective-permute-start(bf16[34,512]{1,0:T(8,128)(2,1)S(1)} %slice_select_fusion.4), channel_id=1, source_target_pairs={{0,2},{2,4},{4,6},{6,8},{8,10},{10,12},{12,14},{14,15},{3,1},{5,3}... | collective-permute-start | bytes 104456 | tf_op jit(solution)/shard_map/ppermute | solution.py:494
  24.6 3.1 %collective-permute-start.6 = (bf16[34,512]{1,0:T(8,128)(2,1)S(1)}, bf16[34,512]{1,0:T(8,128)(2,1)S(1)}, u32[]{:S(2)}, u32[]{:S(2)}) collective-permute-start(bf16[34,512]{1,0:T(8,128)(2,1)S(1)} %collective-permute-done.5), channel_id=1, source_target_pairs={{0,1},{1,0},{2,3},{3,2},{4,5},{5,4},{6,7},{7,6},{8,9},{9,8},{10,11... | collective-permute-start | bytes 104456 | tf_op jit(solution)/shard_map/ppermute | solution.py:485
  34.4 1.3 %collective-permute-start.7 = (bf16[48,256]{1,0:T(8,128)(2,1)S(1)}, bf16[48,256]{1,0:T(8,128)(2,1)S(1)}, u32[]{:S(2)}, u32[]{:S(2)}) collective-permute-start(bf16[48,256]{1,0:T(8,128)(2,1)S(1)} %select_convert_fusion), channel_id=1, source_target_pairs={{0,1},{1,0},{2,3},{3,2},{4,5},{5,4},{6,7},{7,6},{8,9},{9,8},{10,11... | collective-permute-start | bytes 73736 | tf_op jit(solution)/shard_map/ppermute | solution.py:485
where the time goes:
time: 36.5 us; the launch traced here: 36.3 us
  Pallas kernels  16.4 us (45%)
  starting transfers between devices  7.94 us (22%)
  waiting for transfers between devices  6.46 us (18%)
  between operations  3.44 us (9%)
  other arithmetic  1.36 us (4%)
  local copies, waits for them, and re-layouts  0.74 us (2%)
    pallas_call x2, Pallas kernels, strip_gradient(): pl.pallas_call(functools.partial(gradient_body, plan), out_shape=jax.Shap...  13.1 us
    ppermute x6, starting transfers between devices, other_corner(): return lax.ppermute(value, 'corner', [(0, 1), (1, 0)])  5.91 us
    ppermute x2, waiting for transfers between devices, neighbours(): got = lax.ppermute(message, ('tile', 'corner'), cycle)  3.55 us
    ppermute x6, waiting for transfers between devices, other_corner(): return lax.ppermute(value, 'corner', [(0, 1), (1, 0)])  2.9 us
    pallas_call x1, Pallas kernels, kernel_spectra(): pl.pallas_call(functools.partial(spectra_body, plan), out_shape=(jax.Shap...  2.23 us
    ppermute x2, starting transfers between devices, neighbours(): got = lax.ppermute(message, ('tile', 'corner'), cycle)  2.03 us
    pallas_call x1, Pallas kernels, fetch(): pl.pallas_call(fetch_body, out_shape=outs, in_specs=[pl.BlockSpec(memory_...  1.03 us
  transfers between devices with their start and end apart: 8, of which 5 were waited for; matrix products, arithmetic and copies ran while one was open for 3% of the time, Pallas kernels for 24%

commit v1 on v0

--- a/solution.py
+++ b/solution.py
@@ -350,12 +350,12 @@
             lane = slice(t * g, t * g + g)
             prods = [[] for _ in range(GROUP)]
             for a, b, c in chunks:
-                s_re, s_im = s_ref[a:b, lane], s_ref[b:c, lane]
+                s_re, s_im = s_ref[a:b, lane].astype(BF), s_ref[b:c, lane].astype(BF)
                 for part in range(GROUP):
                     k = GROUP * group + part
-                    k_re, k_im = spec_ref[k, a:b], spec_ref[k, b:c]
-                    prods[part].append((s_re * k_re - s_im * k_im).astype(BF))
-                    prods[part].append((s_re * k_im + s_im * k_re).astype(BF))
+                    k_re, k_im = spec_ref[k, a:b].astype(BF), spec_ref[k, b:c].astype(BF)
+                    prods[part].append(s_re * k_re - s_im * k_im)
+                    prods[part].append(s_re * k_im + s_im * k_re)
             block = jnp.concatenate([jnp.concatenate(p, axis=0) for p in prods], axis=1)
             passed.append(dot(plan.table(table_ref, "row_inv"), block))
         stack = []
@@ -382,7 +382,7 @@
         return carry
 
     multiply(0)
-    lax.fori_loop(0, groups - 1, forward, 0)
+    lax.fori_loop(0, groups - 1, forward, 0, unroll=True)
     image(groups - 1)
 
     dose = dose_ref[:1, :1]
@@ -438,7 +438,7 @@
         return carry
 
     image_back(0)
-    lax.fori_loop(0, groups - 1, backward, 0)
+    lax.fori_loop(0, groups - 1, backward, 0, unroll=True)
     multiply_back(groups - 1)
 
     d_along = dot(plan.table(table_ref, "row_adj"), acc_ref[...].astype(BF))

time: 36.5 us -> 33.8 us (0.926)
  the two profiles are of different devices: /device:TPU:21 before, /device:TPU:25 now
where the time goes in v1:
time: 33.8 us; the launch traced here: 33.6 us
  Pallas kernels  13.6 us (40%)
  starting transfers between devices  7.94 us (23%)
  waiting for transfers between devices  6.46 us (19%)
  between operations  3.45 us (10%)
  other arithmetic  1.35 us (4%)
  local copies, waits for them, and re-layouts  0.74 us (2%)
    pallas_call x2, Pallas kernels, strip_gradient(): pl.pallas_call(functools.partial(gradient_body, plan), out_shape=jax.Shap...  10.4 us
    ppermute x6, starting transfers between devices, other_corner(): return lax.ppermute(value, 'corner', [(0, 1), (1, 0)])  5.91 us
    ppermute x2, waiting for transfers between devices, neighbours(): got = lax.ppermute(message, ('tile', 'corner'), cycle)  3.56 us
    ppermute x6, waiting for transfers between devices, other_corner(): return lax.ppermute(value, 'corner', [(0, 1), (1, 0)])  2.9 us
    pallas_call x1, Pallas kernels, kernel_spectra(): pl.pallas_call(functools.partial(spectra_body, plan), out_shape=(jax.Shap...  2.23 us
    ppermute x2, starting transfers between devices, neighbours(): got = lax.ppermute(message, ('tile', 'corner'), cycle)  2.02 us
    pallas_call x1, Pallas kernels, fetch(): pl.pallas_call(fetch_body, out_shape=outs, in_specs=[pl.BlockSpec(memory_...  1.03 us
    sub x1, other arithmetic, per_device(): logits = logits - step_size * first_hat / (jnp.sqrt(second_hat) + adam_eps)  0.69 us
  transfers between devices with their start and end apart: 8, of which 5 were waited for; matrix products, arithmetic and copies ran while one was open for 3% of the time, Pallas kernels for 22%

profile of v1, /device:TPU:25, one launch (start us, length us, event | category | flops | bytes accessed | tf_op | source)
XLA Modules:
  0.0 33.6 jit_solution(11146969750173173352)
XLA Ops:
  0.6 1.0 %fetch.1 = (bf16[48,256]{1,0:T(8,128)(2,1)S(1)}, f32[3,48,256]{2,1,0:T(8,128)S(1)}, bf16[48,512]{1,0:T(8,128)(2,1)S(1)}, f32[8,512]{1,0:T(8,128)S(1)}, f32[3,8,128]{2,1,0:T(8,128)S(1)}) custom-call(f32[48,256]{1,0:T(8,128)} %logits_hbm.1, f32[48,256]{1,0:T(8,128)} %first_hbm.1, f32[48,256]{1,0:T(8,128)} %second_hbm.1, bf16[48,512]{1,0:T(8,128)(2,1)} %target_hbm.1, ...), custom_call_target="tpu_custom_call" | custom-call | tf_op jit(solution)/shard_map/fetch/pallas_call | solution.py:216
  1.7 0.7 %collective-permute-start.1 = (bf16[48,256]{1,0:T(8,128)(2,1)S(1)}, bf16[48,256]{1,0:T(8,128)(2,1)S(1)}, u32[]{:S(2)}, u32[]{:S(2)}) collective-permute-start(bf16[48,256]{1,0:T(8,128)(2,1)S(1)} %get-tuple-element.12), channel_id=1, source_target_pairs={{0,1},{1,0},{2,3},{3,2},{4,5},{5,4},{6,7},{7,6},{8,9},{9,8},{10,11... | collective-permute-start | bytes 73736 | tf_op jit(solution)/shard_map/ppermute | solution.py:485
  2.4 0.5 %fusion.26 = (f32[1,1,1]{2,1,0:T(1,128)}, f32[1,1,1]{2,1,0:T(1,128)}, f32[1,1,1]{2,1,0:T(1,128)}) fusion(f32[3,8,128]{2,1,0:T(8,128)S(1)} %get-tuple-element.10), kind=kLoop, calls=%fused_computation.64 | loop fusion | bytes 24 | tf_op jit(solution)/shard_map/slice | solution.py:528
  3.7 1.2 %collective-permute-start.2 = (bf16[52,512]{1,0:T(8,128)(2,1)S(1)}, bf16[52,512]{1,0:T(8,128)(2,1)S(1)}, u32[]{:S(2)}, u32[]{:S(2)}) collective-permute-start(bf16[52,512]{1,0:T(8,128)(2,1)S(1)} %fusion.11), channel_id=1, source_target_pairs={{0,2},{2,4},{4,6},{6,8},{8,10},{10,12},{12,14},{14,15},{3,1},{5,3}... | collective-permute-start | bytes 159752 | tf_op jit(solution)/shard_map/ppermute | solution.py:494
  4.9 0.4 %collective-permute-start = (f32[3,48,256]{2,1,0:T(8,128)S(1)}, f32[3,48,256]{2,1,0:T(8,128)S(1)}, u32[]{:S(2)}, u32[]{:S(2)}) collective-permute-start(f32[3,48,256]{2,1,0:T(8,128)S(1)} %get-tuple-element.11), channel_id=1, source_target_pairs={{0,1},{1,0},{2,3},{3,2},{4,5},{5,4},{6,7},{7,6},{8,9},{9,8},{10,11... | collective-permute-start | bytes 442376 | tf_op jit(solution)/shard_map/ppermute | solution.py:485
  5.3 1.5 %collective-permute-done.2 = bf16[52,512]{1,0:T(8,128)(2,1)S(1)} collective-permute-done((bf16[52,512]{1,0:T(8,128)(2,1)S(1)}, bf16[52,512]{1,0:T(8,128)(2,1)S(1)}, u32[]{:S(2)}, u32[]{:S(2)}) %collective-permute-start.2) | collective-permute-done | bytes 53280 | tf_op jit(solution)/shard_map/ppermute | solution.py:494
  6.8 2.1 %collective-permute-start.3 = (bf16[52,512]{1,0:T(8,128)(2,1)S(1)}, bf16[52,512]{1,0:T(8,128)(2,1)S(1)}, u32[]{:S(2)}, u32[]{:S(2)}) collective-permute-start(bf16[52,512]{1,0:T(8,128)(2,1)S(1)} %collective-permute-done.2), channel_id=1, source_target_pairs={{0,1},{1,0},{2,3},{3,2},{4,5},{5,4},{6,7},{7,6},{8,9},{9,8},{10,11... | collective-permute-start | bytes 159752 | tf_op jit(solution)/shard_map/ppermute | solution.py:485
  9.6 0.1 pad.20.clone
  11.0 2.2 %spectra.1 = (f32[16,256,128]{2,1,0:T(8,128)S(1)}, f32[16,8,256]{2,1,0:T(8,128)S(1)}) custom-call(f32[1,8]{1,0:T(1,128)} %weight_hbm.1, f32[8,35,2,35]{3,2,1,0:T(2,128)} %bitcast.25, bf16[352,256]{1,0:T(8,128)(2,1)} %constant.16.clone.table_hbm), custom_call_target="tpu_custom_call" | custom-call | tf_op jit(solution)/shard_map/spectra/pallas_call | solution.py:283
  13.2 0.1 select_select_fusion.1
  13.4 0.1 maximum_maximum_fusion.2.target_ref
  13.5 0.1 maximum_maximum_fusion.mask_ref
  13.6 5.2 %gradient.2 = f32[48,512]{1,0:T(8,128)S(1)} custom-call(f32[8,128]{1,0:T(8,128)S(1)} %broadcast_in_dim.152.dose_ref, bf16[128,512]{1,0:T(8,128)(2,1)S(1)} %maximum_maximum_fusion.mask_ref, bf16[88,512]{1,0:T(8,128)(2,1)S(1)} %maximum_maximum_fusion.2.target_ref, f32[8,512]{1,0:T(8,128)S(1)} %add_divide_fusion.1.weight_ref, ...), custom_call_target="tpu_custom_call" | custom-call | tf_op jit(solution)/shard_map/gradient/pallas_call | solution.py:466
  19.0 1.2 %collective-permute-done.4 = bf16[48,512]{1,0:T(8,128)(2,1)S(1)} collective-permute-done((bf16[48,512]{1,0:T(8,128)(2,1)S(1)}, bf16[48,512]{1,0:T(8,128)(2,1)S(1)}, u32[]{:S(2)}, u32[]{:S(2)}) %collective-permute-start.4) | collective-permute-done | bytes 49184 | tf_op jit(solution)/shard_map/ppermute | solution.py:485
  20.1 0.1 add_convert_fusion
  20.3 0.9 %collective-permute-start.5 = (bf16[34,512]{1,0:T(8,128)(2,1)S(1)}, bf16[34,512]{1,0:T(8,128)(2,1)S(1)}, u32[]{:S(2)}, u32[]{:S(2)}) collective-permute-start(bf16[34,512]{1,0:T(8,128)(2,1)S(1)} %slice_select_fusion.4), channel_id=1, source_target_pairs={{0,2},{2,4},{4,6},{6,8},{8,10},{10,12},{12,14},{14,15},{3,1},{5,3}... | collective-permute-start | bytes 104456 | tf_op jit(solution)/shard_map/ppermute | solution.py:494
  21.2 2.0 %collective-permute-done.5 = bf16[34,512]{1,0:T(8,128)(2,1)S(1)} collective-permute-done((bf16[34,512]{1,0:T(8,128)(2,1)S(1)}, bf16[34,512]{1,0:T(8,128)(2,1)S(1)}, u32[]{:S(2)}, u32[]{:S(2)}) %collective-permute-start.5) | collective-permute-done | bytes 34848 | tf_op jit(solution)/shard_map/ppermute | solution.py:494
  23.2 2.2 %collective-permute-start.6 = (bf16[34,512]{1,0:T(8,128)(2,1)S(1)}, bf16[34,512]{1,0:T(8,128)(2,1)S(1)}, u32[]{:S(2)}, u32[]{:S(2)}) collective-permute-start(bf16[34,512]{1,0:T(8,128)(2,1)S(1)} %collective-permute-done.5), channel_id=1, source_target_pairs={{0,1},{1,0},{2,3},{3,2},{4,5},{5,4},{6,7},{7,6},{8,9},{9,8},{10,11... | collective-permute-start | bytes 104456 | tf_op jit(solution)/shard_map/ppermute | solution.py:485
  25.4 0.9 %collective-permute-done.6 = bf16[34,512]{1,0:T(8,128)(2,1)S(1)} collective-permute-done((bf16[34,512]{1,0:T(8,128)(2,1)S(1)}, bf16[34,512]{1,0:T(8,128)(2,1)S(1)}, u32[]{:S(2)}, u32[]{:S(2)}) %collective-permute-start.6) | collective-permute-done | bytes 34848 | tf_op jit(solution)/shard_map/ppermute | solution.py:485
  26.3 0.1 maximum_maximum_fusion.1.mask_ref
  26.4 5.2 %gradient.3 = f32[48,512]{1,0:T(8,128)S(1)} custom-call(f32[8,128]{1,0:T(8,128)S(1)} %broadcast_in_dim.152.dose_ref, bf16[128,512]{1,0:T(8,128)(2,1)S(1)} %maximum_maximum_fusion.1.mask_ref, bf16[88,512]{1,0:T(8,128)(2,1)S(1)} %maximum_maximum_fusion.2.target_ref, f32[8,512]{1,0:T(8,128)S(1)} %add_divide_fusion.1.weight_ref, ...), custom_call_target="tpu_custom_call" | custom-call | tf_op jit(solution)/shard_map/gradient/pallas_call | solution.py:466
  31.6 0.4 %collective-permute-start.7 = (bf16[48,256]{1,0:T(8,128)(2,1)S(1)}, bf16[48,256]{1,0:T(8,128)(2,1)S(1)}, u32[]{:S(2)}, u32[]{:S(2)}) collective-permute-start(bf16[48,256]{1,0:T(8,128)(2,1)S(1)} %select_convert_fusion), channel_id=1, source_target_pairs={{0,1},{1,0},{2,3},{3,2},{4,5},{5,4},{6,7},{7,6},{8,9},{9,8},{10,11... | collective-permute-start | bytes 73736 | tf_op jit(solution)/shard_map/ppermute | solution.py:485
  32.0 0.8 %collective-permute-done.7 = bf16[48,256]{1,0:T(8,128)(2,1)S(1)} collective-permute-done((bf16[48,256]{1,0:T(8,128)(2,1)S(1)}, bf16[48,256]{1,0:T(8,128)(2,1)S(1)}, u32[]{:S(2)}, u32[]{:S(2)}) %collective-permute-start.7) | collective-permute-done | bytes 24608 | tf_op jit(solution)/shard_map/ppermute | solution.py:485
  32.9 0.7 %fusion.18 = (f32[48,256]{1,0:T(8,128)}, f32[48,256]{1,0:T(8,128)}, f32[48,256]{1,0:T(8,128)}) fusion(f32[48,512]{1,0:T(8,128)S(1)} %get-tuple-element.22, pred[]{:T(512)} %bitcast, f32[48,512]{1,0:T(8,128)S(1)} %get-tuple-element.23, f32[48,512]{1,0:T(8,128)S(1)} %get-tuple-element.24, f32[48,512]{1,0:T(8,128)S(1)} %get-tuple-element.21, ...), kind=kLoop, calls=%fused_computation.43 | loop fusion | flops 270336 | bytes 663553 | tf_op jit(solution)/shard_map/sub | solution.py:579
  (28 shorter events, 0.4 us)
Async XLA Ops:
  0.6 13.0 %copy-start = (bf16[2848,256]{1,0:T(8,128)(2,1)S(1)}, bf16[2848,256]{1,0:T(8,128)(2,1)}, u32[]{:S(2)}) copy-start(bf16[2848,256]{1,0:T(8,128)(2,1)} %constant.15.clone.table_ref) | copy-start | bytes 4374532
  1.7 1.9 %collective-permute-start.1 = (bf16[48,256]{1,0:T(8,128)(2,1)S(1)}, bf16[48,256]{1,0:T(8,128)(2,1)S(1)}, u32[]{:S(2)}, u32[]{:S(2)}) collective-permute-start(bf16[48,256]{1,0:T(8,128)(2,1)S(1)} %get-tuple-element.12), channel_id=1, source_target_pairs={{0,1},{1,0},{2,3},{3,2},{4,5},{5,4},{6,7},{7,6},{8,9},{9,8},{10,11... | collective-permute-start | bytes 73736 | tf_op jit(solution)/shard_map/ppermute | solution.py:485
  3.7 3.1 %collective-permute-start.2 = (bf16[52,512]{1,0:T(8,128)(2,1)S(1)}, bf16[52,512]{1,0:T(8,128)(2,1)S(1)}, u32[]{:S(2)}, u32[]{:S(2)}) collective-permute-start(bf16[52,512]{1,0:T(8,128)(2,1)S(1)} %fusion.11), channel_id=1, source_target_pairs={{0,2},{2,4},{4,6},{6,8},{8,10},{10,12},{12,14},{14,15},{3,1},{5,3}... | collective-permute-start | bytes 159752 | tf_op jit(solution)/shard_map/ppermute | solution.py:494
  4.9 14.1 %collective-permute-start = (f32[3,48,256]{2,1,0:T(8,128)S(1)}, f32[3,48,256]{2,1,0:T(8,128)S(1)}, u32[]{:S(2)}, u32[]{:S(2)}) collective-permute-start(f32[3,48,256]{2,1,0:T(8,128)S(1)} %get-tuple-element.11), channel_id=1, source_target_pairs={{0,1},{1,0},{2,3},{3,2},{4,5},{5,4},{6,7},{7,6},{8,9},{9,8},{10,11... | collective-permute-start | bytes 442376 | tf_op jit(solution)/shard_map/ppermute | solution.py:485
  6.8 6.4 %collective-permute-start.3 = (bf16[52,512]{1,0:T(8,128)(2,1)S(1)}, bf16[52,512]{1,0:T(8,128)(2,1)S(1)}, u32[]{:S(2)}, u32[]{:S(2)}) collective-permute-start(bf16[52,512]{1,0:T(8,128)(2,1)S(1)} %collective-permute-done.2), channel_id=1, source_target_pairs={{0,1},{1,0},{2,3},{3,2},{4,5},{5,4},{6,7},{7,6},{8,9},{9,8},{10,11... | collective-permute-start | bytes 159752 | tf_op jit(solution)/shard_map/ppermute | solution.py:485
  18.8 1.3 %collective-permute-start.4 = (bf16[48,512]{1,0:T(8,128)(2,1)S(1)}, bf16[48,512]{1,0:T(8,128)(2,1)S(1)}, u32[]{:S(2)}, u32[]{:S(2)}) collective-permute-start(bf16[48,512]{1,0:T(8,128)(2,1)S(1)} %convert_element_type.40), channel_id=1, source_target_pairs={{0,1},{1,0},{2,3},{3,2},{4,5},{5,4},{6,7},{7,6},{8,9},{9,8},{10,11... | collective-permute-start | bytes 147464 | tf_op jit(solution)/shard_map/ppermute | solution.py:485
  20.3 2.9 %collective-permute-start.5 = (bf16[34,512]{1,0:T(8,128)(2,1)S(1)}, bf16[34,512]{1,0:T(8,128)(2,1)S(1)}, u32[]{:S(2)}, u32[]{:S(2)}) collective-permute-start(bf16[34,512]{1,0:T(8,128)(2,1)S(1)} %slice_select_fusion.4), channel_id=1, source_target_pairs={{0,2},{2,4},{4,6},{6,8},{8,10},{10,12},{12,14},{14,15},{3,1},{5,3}... | collective-permute-start | bytes 104456 | tf_op jit(solution)/shard_map/ppermute | solution.py:494
  23.2 3.1 %collective-permute-start.6 = (bf16[34,512]{1,0:T(8,128)(2,1)S(1)}, bf16[34,512]{1,0:T(8,128)(2,1)S(1)}, u32[]{:S(2)}, u32[]{:S(2)}) collective-permute-start(bf16[34,512]{1,0:T(8,128)(2,1)S(1)} %collective-permute-done.5), channel_id=1, source_target_pairs={{0,1},{1,0},{2,3},{3,2},{4,5},{5,4},{6,7},{7,6},{8,9},{9,8},{10,11... | collective-permute-start | bytes 104456 | tf_op jit(solution)/shard_map/ppermute | solution.py:485
  31.6 1.3 %collective-permute-start.7 = (bf16[48,256]{1,0:T(8,128)(2,1)S(1)}, bf16[48,256]{1,0:T(8,128)(2,1)S(1)}, u32[]{:S(2)}, u32[]{:S(2)}) collective-permute-start(bf16[48,256]{1,0:T(8,128)(2,1)S(1)} %select_convert_fusion), channel_id=1, source_target_pairs={{0,1},{1,0},{2,3},{3,2},{4,5},{5,4},{6,7},{7,6},{8,9},{9,8},{10,11... | collective-permute-start | bytes 73736 | tf_op jit(solution)/shard_map/ppermute | solution.py:485

commit v2 on v1

--- a/solution.py
+++ b/solution.py
@@ -169,12 +169,19 @@
     second_hbm,
     target_hbm,
     counts_hbm,
+    taps_hbm,
+    tables_hbm,
+    socs_hbm,
     mask_ref,
     state_ref,
     target_ref,
     counts_ref,
     flags_ref,
+    taps_ref,
+    tables_ref,
+    roots_ref,
     counts_smem,
+    socs_smem,
     sems,
 ):
     pairs = (
@@ -183,6 +190,9 @@
         (target_hbm, target_ref),
         (first_hbm, state_ref.at[1]),
         (second_hbm, state_ref.at[2]),
+        (taps_hbm, taps_ref),
+        (tables_hbm, tables_ref),
+        (socs_hbm, socs_smem),
     )
     copies = [pltpu.make_async_copy(a, b, sems.at[i]) for i, (a, b) in enumerate(pairs)]
     for copy in copies:
@@ -190,12 +200,14 @@
     place, corner = lax.axis_index("tile"), lax.axis_index("corner")
     facts = (corner == 0, place == 0, place == lax.axis_size("tile") - 1)
     for i, fact in enumerate(facts):
-        flags_ref[i] = jnp.full((8, LANES), jnp.where(fact, 1.0, 0.0), F32)
+        flags_ref[i] = jnp.full(flags_ref.shape[1:], jnp.where(fact, 1.0, 0.0), F32)
     copies[0].wait()
     mask = (1.0 / (1.0 + jnp.exp(-state_ref[0]))).astype(BF)
     mask_ref[...] = (mask.astype(F32) - MIDDLE).astype(BF)
     for copy in copies[1:]:
         copy.wait()
+    for k in range(roots_ref.shape[0]):
+        roots_ref[k] = jnp.sqrt(jnp.full(roots_ref.shape[1:], socs_smem[0, k], F32))
     tiles = counts_smem.shape[1]
     wide = counts_ref.shape[1] // tiles
     for tile in range(tiles):
@@ -203,15 +215,22 @@
         counts_ref[:, tile * wide : (tile + 1) * wide] = jnp.full((8, wide), value, F32)
 
 
-def fetch(mask_logits, adam_first, adam_second, target, tile_counts):
-    args = (mask_logits, adam_first, adam_second, target, tile_counts)
+def fetch(
+    flag_rows, mask_logits, adam_first, adam_second, target, tile_counts, taps, tables, socs_weight
+):
+    args = (
+        mask_logits, adam_first, adam_second, target, tile_counts, taps, tables, socs_weight
+    )
     shape = mask_logits.shape
     outs = (
         jax.ShapeDtypeStruct(shape, BF),
         jax.ShapeDtypeStruct((3,) + shape, F32),
         jax.ShapeDtypeStruct(target.shape, BF),
         jax.ShapeDtypeStruct((8, target.shape[1]), F32),
-        jax.ShapeDtypeStruct((3, 8, LANES), F32),
+        jax.ShapeDtypeStruct((3, flag_rows, target.shape[1]), F32),
+        jax.ShapeDtypeStruct(taps.shape, F32),
+        jax.ShapeDtypeStruct(tables.shape, BF),
+        jax.ShapeDtypeStruct((socs_weight.shape[1], 8, COL_LEN), F32),
     )
     return pl.pallas_call(
         fetch_body,
@@ -220,6 +239,7 @@
         out_specs=tuple(pl.BlockSpec(memory_space=pltpu.VMEM) for _ in outs),
         scratch_shapes=[
             pltpu.SMEM(tile_counts.shape, jnp.int32),
+            pltpu.SMEM(socs_weight.shape, F32),
             pltpu.SemaphoreType.DMA((len(args),)),
         ],
         compiler_params=pltpu.CompilerParams(vmem_limit_bytes=4 * 1024 * 1024),
@@ -227,27 +247,7 @@
     )(*(pltpu.with_memory_space_constraint(value, pltpu.HBM) for value in args))
 
 
-def spectra_body(
-    plan,
-    weight_hbm,
-    kern_hbm,
-    table_hbm,
-    out_ref,
-    level_ref,
-    weight_ref,
-    kern_ref,
-    table_ref,
-    sems,
-):
-    copies = [
-        pltpu.make_async_copy(kern_hbm, kern_ref, sems.at[0]),
-        pltpu.make_async_copy(table_hbm, table_ref, sems.at[1]),
-        pltpu.make_async_copy(weight_hbm, weight_ref, sems.at[2]),
-    ]
-    for copy in copies:
-        copy.start()
-    for copy in copies:
-        copy.wait()
+def spectra_body(plan, root_ref, kern_ref, table_ref, out_ref, level_ref):
     count = out_ref.shape[0]
     pad = plan.taps_pad - plan.taps
     stack, sums = [], []
@@ -267,7 +267,7 @@
             both.append(jnp.concatenate([one[:, :HALF_SPEC], one[:, HALF_SPEC:]], axis=0))
         hi, lo = split(jnp.concatenate(both, axis=1))
         spec = dot(plan.table(table_ref, "tap_rows"), jnp.concatenate([hi, hi, lo], axis=0))
-        root_wide = jnp.sqrt(jnp.full((8, COL_LEN), weight_ref[0, k // 2], F32))
+        root_wide = root_ref[k // 2]
         root = root_wide[:1, :HALF_SPEC]
         for part in (k, k + 1):
             level_ref[part] = root_wide * sums[part : part + 1]
@@ -275,33 +275,20 @@
         out_ref[k + 1] = spec[:, HALF_SPEC:] * root
 
 
-def kernel_spectra(plan, kernels, socs_weight):
-    count = kernels.shape[1] * kernels.shape[2]
-    taps = kernels[0].transpose(0, 2, 1, 3)
-    tables = plan.tap_packed
-    hbm = pl.BlockSpec(memory_space=pltpu.HBM)
+def kernel_spectra(plan, taps, tables, roots):
+    count = 2 * taps.shape[0]
+    vmem = pl.BlockSpec(memory_space=pltpu.VMEM)
     return pl.pallas_call(
         functools.partial(spectra_body, plan),
         out_shape=(
             jax.ShapeDtypeStruct((count, 2 * plan.row_len, HALF_SPEC), F32),
             jax.ShapeDtypeStruct((count, 8, COL_LEN), F32),
         ),
-        in_specs=[hbm] * 3,
-        out_specs=(pl.BlockSpec(memory_space=pltpu.VMEM), pl.BlockSpec(memory_space=pltpu.VMEM)),
-        scratch_shapes=[
-            pltpu.SMEM(socs_weight.shape, F32),
-            pltpu.VMEM(taps.shape, F32),
-            pltpu.VMEM(tables.shape, BF),
-            pltpu.SemaphoreType.DMA((3,)),
-        ],
+        in_specs=[vmem] * 3,
+        out_specs=(vmem, vmem),
         compiler_params=pltpu.CompilerParams(vmem_limit_bytes=4 * 1024 * 1024),
         name="spectra",
-    )(
-        *(
-            pltpu.with_memory_space_constraint(value, pltpu.HBM)
-            for value in (socs_weight, taps, jnp.asarray(tables))
-        ),
-    )
+    )(roots, taps, tables)
 
 
 def gradient_body(
@@ -487,7 +474,7 @@
 
 def neighbours(flags, top, bottom, blank):
     strips = lax.axis_size("tile")
-    first_corner, highest, lowest = flags
+    first_corner, highest, lowest = flags[:, : top.shape[0], : top.shape[1]]
     cycle = [(2 * i, 2 * i + 2) for i in range(strips - 1)] + [(2 * strips - 2, 2 * strips - 1)]
     cycle += [(2 * i + 1, 2 * i - 1) for i in range(1, strips)] + [(1, 0)]
     message = jnp.where(first_corner, bottom, top)
@@ -508,11 +495,13 @@
     halo = 2 * reach
 
     def whole(own, other):
+        first_corner = flags[0, : own.shape[-2], : own.shape[-1]]
         left = jnp.where(first_corner, own, other)
         right = jnp.where(first_corner, other, own)
         return jnp.concatenate([left, right], axis=-1)
 
     def own_half(value):
+        first_corner = flags[0, : value.shape[-2], :half_width]
         return jnp.where(first_corner, value[..., :half_width], value[..., half_width:])
 
     def extended(above_rows, own, below_rows, total):
@@ -522,11 +511,18 @@
 
     tables = jnp.asarray(plan.packed)
 
-    mask_half, state, target, counts, facts = fetch(
-        mask_logits, adam_first, adam_second, target, tile_counts
-    )
-    flags = [facts[i, :1, :1] > 0.5 for i in range(3)]
-    first_corner = flags[0]
+    mask_half, state, target, counts, facts, taps, tap_tables, roots = fetch(
+        up_to(max(strip_rows, halo + reach + 1), 8),
+        mask_logits,
+        adam_first,
+        adam_second,
+        target,
+        tile_counts,
+        kernels[0].transpose(0, 2, 1, 3),
+        jnp.asarray(plan.tap_packed),
+        socs_weight,
+    )
+    flags = facts > 0.5
     dose = jnp.broadcast_to(corner_dose[None], (8, LANES))
     counts = counts[:1]
     counts_bf = counts.astype(BF)
@@ -538,7 +534,7 @@
         jnp.concatenate([mask_bf[-halo:], target[-reach:], counts_bf], axis=0),
         jnp.where(jnp.arange(halo + reach + 1)[:, None] < halo, -MIDDLE, 0.0).astype(BF),
     )
-    spec = kernel_spectra(plan, kernels, socs_weight)
+    spec = kernel_spectra(plan, taps, tap_tables, roots)
     target_ext = extended(
         above[halo : halo + reach], target, below[halo : halo + reach], plan.field_pad
     )
@@ -566,7 +562,7 @@
             summed = partial + other_corner(partial.astype(BF)).astype(F32)
         else:
             mine = own_half(partial)
-            theirs = jnp.where(first_corner, partial[:, half_width:], partial[:, :half_width])
+            theirs = jnp.where(flags[0, :strip_rows, :half_width], partial[:, half_width:], partial[:, :half_width])
             summed = mine + other_corner(theirs.astype(BF)).astype(F32)
             opacity, logits = own_half(opacity), own_half(logits)
             first, second = own_half(first), own_half(second)

time: 33.8 us -> 31.6 us (0.935)
  the two profiles are of different devices: /device:TPU:25 before, /device:TPU:9 now
where the time goes in v2:
time: 31.6 us; the launch traced here: 31.5 us
  Pallas kernels  12.9 us (41%)
  starting transfers between devices  7.94 us (25%)
  waiting for transfers between devices  7.55 us (24%)
  between operations  1.49 us (5%)
  other arithmetic  1.43 us (5%)
    pallas_call x2, Pallas kernels, strip_gradient(): pl.pallas_call(functools.partial(gradient_body, plan), out_shape=jax.Shap...  10.4 us
    ppermute x6, starting transfers between devices, other_corner(): return lax.ppermute(value, 'corner', [(0, 1), (1, 0)])  5.92 us
    ppermute x2, waiting for transfers between devices, neighbours(): got = lax.ppermute(message, ('tile', 'corner'), cycle)  3.97 us
    ppermute x6, waiting for transfers between devices, other_corner(): return lax.ppermute(value, 'corner', [(0, 1), (1, 0)])  3.58 us
    ppermute x2, starting transfers between devices, neighbours(): got = lax.ppermute(message, ('tile', 'corner'), cycle)  2.02 us
    pallas_call x1, Pallas kernels, fetch(): pl.pallas_call(fetch_body, out_shape=outs, in_specs=[pl.BlockSpec(memory_...  1.31 us
    pallas_call x1, Pallas kernels, kernel_spectra(): pl.pallas_call(functools.partial(spectra_body, plan), out_shape=(jax.Shap...  1.19 us
    sub x1, other arithmetic, per_device(): logits = logits - step_size * first_hat / (jnp.sqrt(second_hat) + adam_eps)  0.69 us
  transfers between devices with their start and end apart: 8, of which 6 were waited for; matrix products, arithmetic and copies ran while one was open for 2% of the time, Pallas kernels for 20%

profile of v2, /device:TPU:9, one launch (start us, length us, event | category | flops | bytes accessed | tf_op | source)
XLA Modules:
  0.0 31.5 jit_solution(1207271085509485564)
XLA Ops:
  0.6 1.3 %fetch.1 = (bf16[48,256]{1,0:T(8,128)(2,1)S(1)}, f32[3,48,256]{2,1,0:T(8,128)S(1)}, bf16[48,512]{1,0:T(8,128)(2,1)S(1)}, f32[8,512]{1,0:T(8,128)S(1)}, f32[3,56,...) custom-call(f32[48,256]{1,0:T(8,128)} %logits_hbm.1, ...), custom_call_target="tpu_custom_call" | custom-call | tf_op jit(solution)/shard_map/fetch/pallas_call | solution.py:235
  2.0 0.7 %collective-permute-start.1 = (bf16[48,256]{1,0:T(8,128)(2,1)S(1)}, bf16[48,256]{1,0:T(8,128)(2,1)S(1)}, u32[]{:S(2)}, u32[]{:S(2)}) collective-permute-start(bf16[48,256]{1,0:T(8,128)(2,1)S(1)} %get-tuple-element.15), channel_id=1, source_target_pairs={{0,1},{1,0},{2,3},{3,2},{4,5},{5,4},{6,7},{7,6},{8,9},{9,8},{10,11... | collective-permute-start | bytes 73736 | tf_op jit(solution)/shard_map/ppermute | solution.py:472
  2.7 0.1 collective-permute-start
  2.9 0.7 %collective-permute-done.1 = bf16[48,256]{1,0:T(8,128)(2,1)S(1)} collective-permute-done((bf16[48,256]{1,0:T(8,128)(2,1)S(1)}, bf16[48,256]{1,0:T(8,128)(2,1)S(1)}, u32[]{:S(2)}, u32[]{:S(2)}) %collective-permute-start.1) | collective-permute-done | bytes 24608 | tf_op jit(solution)/shard_map/ppermute | solution.py:472
  3.6 1.2 %collective-permute-start.2 = (bf16[52,512]{1,0:T(8,128)(2,1)S(1)}, bf16[52,512]{1,0:T(8,128)(2,1)S(1)}, u32[]{:S(2)}, u32[]{:S(2)}) collective-permute-start(bf16[52,512]{1,0:T(8,128)(2,1)S(1)} %fusion.17), channel_id=1, source_target_pairs={{0,2},{2,4},{4,6},{6,8},{8,10},{10,12},{12,14},{14,15},{3,1},{5,3}... | collective-permute-start | bytes 159752 | tf_op jit(solution)/shard_map/ppermute | solution.py:481
  4.8 1.9 %collective-permute-done.2 = bf16[52,512]{1,0:T(8,128)(2,1)S(1)} collective-permute-done((bf16[52,512]{1,0:T(8,128)(2,1)S(1)}, bf16[52,512]{1,0:T(8,128)(2,1)S(1)}, u32[]{:S(2)}, u32[]{:S(2)}) %collective-permute-start.2) | collective-permute-done | bytes 53280 | tf_op jit(solution)/shard_map/ppermute | solution.py:481
  6.7 2.4 %collective-permute-start.3 = (bf16[52,512]{1,0:T(8,128)(2,1)S(1)}, bf16[52,512]{1,0:T(8,128)(2,1)S(1)}, u32[]{:S(2)}, u32[]{:S(2)}) collective-permute-start(bf16[52,512]{1,0:T(8,128)(2,1)S(1)} %collective-permute-done.2), channel_id=1, source_target_pairs={{0,1},{1,0},{2,3},{3,2},{4,5},{5,4},{6,7},{7,6},{8,9},{9,8},{10,11... | collective-permute-start | bytes 159752 | tf_op jit(solution)/shard_map/ppermute | solution.py:472
  9.2 0.1 pad.20.clone
  9.9 1.2 %spectra.1 = (f32[16,256,128]{2,1,0:T(8,128)S(1)}, f32[16,8,256]{2,1,0:T(8,128)S(1)}) custom-call(f32[8,8,256]{2,1,0:T(8,128)S(1)} %get-tuple-element.18.root_ref, f32[8,35,2,35]{3,2,1,0:T(2,128)S(1)} %get-tuple-element.19.kern_ref, bf16[352,256]{1,0:T(8,128)(2,1)S(1)} %get-tuple-element.20.table_ref), custom_call_target="tpu_custom_call" | custom-call | tf_op jit(solution)/shard_map/spectra/pallas_call | solution.py:281
  11.1 0.1 fusion.3
  11.3 0.1 maximum_maximum_fusion.2.target_ref
  11.4 0.1 maximum_maximum_fusion.mask_ref
  11.5 5.2 %gradient.2 = f32[48,512]{1,0:T(8,128)S(1)} custom-call(f32[8,128]{1,0:T(8,128)S(1)} %broadcast_in_dim.52.dose_ref, bf16[128,512]{1,0:T(8,128)(2,1)S(1)} %maximum_maximum_fusion.mask_ref, bf16[88,512]{1,0:T(8,128)(2,1)S(1)} %maximum_maximum_fusion.2.target_ref, f32[8,512]{1,0:T(8,128)S(1)} %add_divide_fusion.1.weight_ref, ...), custom_call_target="tpu_custom_call" | custom-call | tf_op jit(solution)/shard_map/gradient/pallas_call | solution.py:453
  16.9 1.2 %collective-permute-done.4 = bf16[48,512]{1,0:T(8,128)(2,1)S(1)} collective-permute-done((bf16[48,512]{1,0:T(8,128)(2,1)S(1)}, bf16[48,512]{1,0:T(8,128)(2,1)S(1)}, u32[]{:S(2)}, u32[]{:S(2)}) %collective-permute-start.4) | collective-permute-done | bytes 49184 | tf_op jit(solution)/shard_map/ppermute | solution.py:472
  18.0 0.1 add_convert_fusion
  18.2 0.9 %collective-permute-start.5 = (bf16[34,512]{1,0:T(8,128)(2,1)S(1)}, bf16[34,512]{1,0:T(8,128)(2,1)S(1)}, u32[]{:S(2)}, u32[]{:S(2)}) collective-permute-start(bf16[34,512]{1,0:T(8,128)(2,1)S(1)} %fusion.27), channel_id=1, source_target_pairs={{0,2},{2,4},{4,6},{6,8},{8,10},{10,12},{12,14},{14,15},{3,1},{5,3}... | collective-permute-start | bytes 104456 | tf_op jit(solution)/shard_map/ppermute | solution.py:481
  19.1 2.0 %collective-permute-done.5 = bf16[34,512]{1,0:T(8,128)(2,1)S(1)} collective-permute-done((bf16[34,512]{1,0:T(8,128)(2,1)S(1)}, bf16[34,512]{1,0:T(8,128)(2,1)S(1)}, u32[]{:S(2)}, u32[]{:S(2)}) %collective-permute-start.5) | collective-permute-done | bytes 34848 | tf_op jit(solution)/shard_map/ppermute | solution.py:481
  21.1 2.2 %collective-permute-start.6 = (bf16[34,512]{1,0:T(8,128)(2,1)S(1)}, bf16[34,512]{1,0:T(8,128)(2,1)S(1)}, u32[]{:S(2)}, u32[]{:S(2)}) collective-permute-start(bf16[34,512]{1,0:T(8,128)(2,1)S(1)} %collective-permute-done.5), channel_id=1, source_target_pairs={{0,1},{1,0},{2,3},{3,2},{4,5},{5,4},{6,7},{7,6},{8,9},{9,8},{10,11... | collective-permute-start | bytes 104456 | tf_op jit(solution)/shard_map/ppermute | solution.py:472
  23.3 0.9 %collective-permute-done.6 = bf16[34,512]{1,0:T(8,128)(2,1)S(1)} collective-permute-done((bf16[34,512]{1,0:T(8,128)(2,1)S(1)}, bf16[34,512]{1,0:T(8,128)(2,1)S(1)}, u32[]{:S(2)}, u32[]{:S(2)}) %collective-permute-start.6) | collective-permute-done | bytes 34848 | tf_op jit(solution)/shard_map/ppermute | solution.py:472
  24.2 0.1 maximum_maximum_fusion.1.mask_ref
  24.3 5.2 %gradient.3 = f32[48,512]{1,0:T(8,128)S(1)} custom-call(f32[8,128]{1,0:T(8,128)S(1)} %broadcast_in_dim.52.dose_ref, bf16[128,512]{1,0:T(8,128)(2,1)S(1)} %maximum_maximum_fusion.1.mask_ref, bf16[88,512]{1,0:T(8,128)(2,1)S(1)} %maximum_maximum_fusion.2.target_ref, f32[8,512]{1,0:T(8,128)S(1)} %add_divide_fusion.1.weight_ref, ...), custom_call_target="tpu_custom_call" | custom-call | tf_op jit(solution)/shard_map/gradient/pallas_call | solution.py:453
  29.5 0.4 %collective-permute-start.7 = (bf16[48,256]{1,0:T(8,128)(2,1)S(1)}, bf16[48,256]{1,0:T(8,128)(2,1)S(1)}, u32[]{:S(2)}, u32[]{:S(2)}) collective-permute-start(bf16[48,256]{1,0:T(8,128)(2,1)S(1)} %select_convert_fusion), channel_id=1, source_target_pairs={{0,1},{1,0},{2,3},{3,2},{4,5},{5,4},{6,7},{7,6},{8,9},{9,8},{10,11... | collective-permute-start | bytes 73736 | tf_op jit(solution)/shard_map/ppermute | solution.py:472
  29.9 0.8 %collective-permute-done.7 = bf16[48,256]{1,0:T(8,128)(2,1)S(1)} collective-permute-done((bf16[48,256]{1,0:T(8,128)(2,1)S(1)}, bf16[48,256]{1,0:T(8,128)(2,1)S(1)}, u32[]{:S(2)}, u32[]{:S(2)}) %collective-permute-start.7) | collective-permute-done | bytes 24608 | tf_op jit(solution)/shard_map/ppermute | solution.py:472
  30.8 0.7 %fusion.24 = (f32[48,256]{1,0:T(8,128)}, f32[48,256]{1,0:T(8,128)}, f32[48,256]{1,0:T(8,128)}) fusion(f32[48,512]{1,0:T(8,128)S(1)} %get-tuple-element.28, pred[3,56,512]{2,1,0:T(8,128)(4,1)S(1)} %broadcast_compare_fusion, f32[48,512]{1,0:T(8,128)S(1)} %get-tuple-element.29, f32[48,512]{1,0:T(8,128)S(1)} %get-tuple-element.30, ...), kind=kLoop, calls=%fused_computation.54 | loop fusion | flops 270336 | bytes 675840 | tf_op jit(solution)/shard_map/sub | solution.py:575
  (29 shorter events, 0.5 us)
Async XLA Ops:
  0.6 10.9 %copy-start = (bf16[2848,256]{1,0:T(8,128)(2,1)S(1)}, bf16[2848,256]{1,0:T(8,128)(2,1)}, u32[]{:S(2)}) copy-start(bf16[2848,256]{1,0:T(8,128)(2,1)} %constant.12.clone.table_ref) | copy-start | bytes 4374532
  2.0 1.6 %collective-permute-start.1 = (bf16[48,256]{1,0:T(8,128)(2,1)S(1)}, bf16[48,256]{1,0:T(8,128)(2,1)S(1)}, u32[]{:S(2)}, u32[]{:S(2)}) collective-permute-start(bf16[48,256]{1,0:T(8,128)(2,1)S(1)} %get-tuple-element.15), channel_id=1, source_target_pairs={{0,1},{1,0},{2,3},{3,2},{4,5},{5,4},{6,7},{7,6},{8,9},{9,8},{10,11... | collective-permute-start | bytes 73736 | tf_op jit(solution)/shard_map/ppermute | solution.py:472
  2.7 14.1 %collective-permute-start = (f32[3,48,256]{2,1,0:T(8,128)S(1)}, f32[3,48,256]{2,1,0:T(8,128)S(1)}, u32[]{:S(2)}, u32[]{:S(2)}) collective-permute-start(f32[3,48,256]{2,1,0:T(8,128)S(1)} %get-tuple-element.14), channel_id=1, source_target_pairs={{0,1},{1,0},{2,3},{3,2},{4,5},{5,4},{6,7},{7,6},{8,9},{9,8},{10,11... | collective-permute-start | bytes 442376 | tf_op jit(solution)/shard_map/ppermute | solution.py:472
  3.6 3.1 %collective-permute-start.2 = (bf16[52,512]{1,0:T(8,128)(2,1)S(1)}, bf16[52,512]{1,0:T(8,128)(2,1)S(1)}, u32[]{:S(2)}, u32[]{:S(2)}) collective-permute-start(bf16[52,512]{1,0:T(8,128)(2,1)S(1)} %fusion.17), channel_id=1, source_target_pairs={{0,2},{2,4},{4,6},{6,8},{8,10},{10,12},{12,14},{14,15},{3,1},{5,3}... | collective-permute-start | bytes 159752 | tf_op jit(solution)/shard_map/ppermute | solution.py:481
  6.7 4.4 %collective-permute-start.3 = (bf16[52,512]{1,0:T(8,128)(2,1)S(1)}, bf16[52,512]{1,0:T(8,128)(2,1)S(1)}, u32[]{:S(2)}, u32[]{:S(2)}) collective-permute-start(bf16[52,512]{1,0:T(8,128)(2,1)S(1)} %collective-permute-done.2), channel_id=1, source_target_pairs={{0,1},{1,0},{2,3},{3,2},{4,5},{5,4},{6,7},{7,6},{8,9},{9,8},{10,11... | collective-permute-start | bytes 159752 | tf_op jit(solution)/shard_map/ppermute | solution.py:472
  16.7 1.3 %collective-permute-start.4 = (bf16[48,512]{1,0:T(8,128)(2,1)S(1)}, bf16[48,512]{1,0:T(8,128)(2,1)S(1)}, u32[]{:S(2)}, u32[]{:S(2)}) collective-permute-start(bf16[48,512]{1,0:T(8,128)(2,1)S(1)} %convert_element_type.40), channel_id=1, source_target_pairs={{0,1},{1,0},{2,3},{3,2},{4,5},{5,4},{6,7},{7,6},{8,9},{9,8},{10,11... | collective-permute-start | bytes 147464 | tf_op jit(solution)/shard_map/ppermute | solution.py:472
  18.2 2.9 %collective-permute-start.5 = (bf16[34,512]{1,0:T(8,128)(2,1)S(1)}, bf16[34,512]{1,0:T(8,128)(2,1)S(1)}, u32[]{:S(2)}, u32[]{:S(2)}) collective-permute-start(bf16[34,512]{1,0:T(8,128)(2,1)S(1)} %fusion.27), channel_id=1, source_target_pairs={{0,2},{2,4},{4,6},{6,8},{8,10},{10,12},{12,14},{14,15},{3,1},{5,3}... | collective-permute-start | bytes 104456 | tf_op jit(solution)/shard_map/ppermute | solution.py:481
  21.1 3.1 %collective-permute-start.6 = (bf16[34,512]{1,0:T(8,128)(2,1)S(1)}, bf16[34,512]{1,0:T(8,128)(2,1)S(1)}, u32[]{:S(2)}, u32[]{:S(2)}) collective-permute-start(bf16[34,512]{1,0:T(8,128)(2,1)S(1)} %collective-permute-done.5), channel_id=1, source_target_pairs={{0,1},{1,0},{2,3},{3,2},{4,5},{5,4},{6,7},{7,6},{8,9},{9,8},{10,11... | collective-permute-start | bytes 104456 | tf_op jit(solution)/shard_map/ppermute | solution.py:472
  29.5 1.3 %collective-permute-start.7 = (bf16[48,256]{1,0:T(8,128)(2,1)S(1)}, bf16[48,256]{1,0:T(8,128)(2,1)S(1)}, u32[]{:S(2)}, u32[]{:S(2)}) collective-permute-start(bf16[48,256]{1,0:T(8,128)(2,1)S(1)} %select_convert_fusion), channel_id=1, source_target_pairs={{0,1},{1,0},{2,3},{3,2},{4,5},{5,4},{6,7},{7,6},{8,9},{9,8},{10,11... | collective-permute-start | bytes 73736 | tf_op jit(solution)/shard_map/ppermute | solution.py:472

commit v3 on v2

--- a/solution.py
+++ b/solution.py
@@ -26,7 +26,7 @@
 MIDDLE = 0.5
 COL_LEN = 2 * HALF_SPEC
 CHUNK = 16
-GROUP = 2
+GROUP = 4
 
 BF = jnp.bfloat16
 F32 = jnp.float32
@@ -388,25 +388,25 @@
         factor = 4.0 * loss_scale * steep * dose
         light_ref[t] = factor * weight * missed * resist * (1.0 - resist)
 
-    def image_back(group):
+    def image_back(group, chosen):
         stack = []
-        for t in range(tiles):
+        for t in chosen:
             for part in range(GROUP):
                 at = (GROUP * t + part) * fr
                 stack.append(light_ref[t] * field_ref[group, at : at + fr])
         inner = dot(jnp.concatenate(stack, axis=0).astype(BF), plan.table(table_ref, "col_inv_adj"))
-        for t in range(tiles):
+        for i, t in enumerate(chosen):
             block = []
             for part in range(GROUP):
-                at = (GROUP * t + part) * fr
+                at = (GROUP * i + part) * fr
                 d = inner[at : at + fr]
                 block.append(jnp.concatenate([d[:, :g], d[:, g:]], axis=0))
-            back_ref[group % 2, t] = jnp.concatenate(block, axis=1).astype(BF)
-
-    def multiply_back(group):
-        for t in range(tiles):
+            back_ref[group % 4, t] = jnp.concatenate(block, axis=1).astype(BF)
+
+    def multiply_back(group, chosen):
+        for t in chosen:
             lane = slice(t * g, t * g + g)
-            d_prod = dot(plan.table(table_ref, "row_inv_adj"), back_ref[group % 2, t])
+            d_prod = dot(plan.table(table_ref, "row_inv_adj"), back_ref[group % 4, t])
             for a, b, c in chunks:
                 sum_re, sum_im = acc_ref[a:b, lane], acc_ref[b:c, lane]
                 for part in range(GROUP):
@@ -419,14 +419,12 @@
                 acc_ref[a:b, lane] = sum_re
                 acc_ref[b:c, lane] = sum_im
 
-    def backward(group, carry):
-        multiply_back(group)
-        image_back(group + 1)
-        return carry
-
-    image_back(0)
-    lax.fori_loop(0, groups - 1, backward, 0, unroll=True)
-    multiply_back(groups - 1)
+    for group in range(1):
+        image_back(group, range(tiles))
+    for group in range(groups):
+        if group + 1 < groups:
+            image_back(group + 1, range(tiles))
+        multiply_back(group, range(tiles))
 
     d_along = dot(plan.table(table_ref, "row_adj"), acc_ref[...].astype(BF))
     parts = []
@@ -461,7 +459,7 @@
             pltpu.VMEM(image, F32),
             pltpu.VMEM(spectrum, F32),
             pltpu.VMEM((2, GROUP * plan.col_tiles * plan.field_pad, COL_LEN), BF),
-            pltpu.VMEM((2, plan.col_tiles, 2 * plan.field_pad, GROUP * HALF_SPEC), BF),
+            pltpu.VMEM((4, plan.col_tiles, 2 * plan.field_pad, GROUP * HALF_SPEC), BF),
         ],
         compiler_params=pltpu.CompilerParams(vmem_limit_bytes=12 * 1024 * 1024),
         name="gradient",

time: 31.6 us -> 29.7 us (0.940)
  Pallas kernels: 12.9 us -> 11 us
    pallas_call x2, Pallas kernels: 10.4 us -> 8.48 us  [strip_gradient(): pl.pallas_call(functools.partial(gradient_body, plan), out_shape=jax.Shap...]
  transfers between devices with their start and end apart: 8 -> 8, of which waited for: 6 -> 6; matrix products, arithmetic and copies ran while one was open for 2% -> 2% of each run, Pallas kernels for 20% -> 18%
where the time goes in v3:
time: 29.7 us; the launch traced here: 29.6 us
  Pallas kernels  11 us (37%)
  starting transfers between devices  7.94 us (27%)
  waiting for transfers between devices  7.55 us (25%)
  between operations  1.48 us (5%)
  other arithmetic  1.43 us (5%)
    pallas_call x2, Pallas kernels, strip_gradient(): pl.pallas_call(functools.partial(gradient_body, plan), out_shape=jax.Shap...  8.48 us
    ppermute x6, starting transfers between devices, other_corner(): return lax.ppermute(value, 'corner', [(0, 1), (1, 0)])  5.91 us
    ppermute x2, waiting for transfers between devices, neighbours(): got = lax.ppermute(message, ('tile', 'corner'), cycle)  3.97 us
    ppermute x6, waiting for transfers between devices, other_corner(): return lax.ppermute(value, 'corner', [(0, 1), (1, 0)])  3.58 us
    ppermute x2, starting transfers between devices, neighbours(): got = lax.ppermute(message, ('tile', 'corner'), cycle)  2.02 us
    pallas_call x1, Pallas kernels, fetch(): pl.pallas_call(fetch_body, out_shape=outs, in_specs=[pl.BlockSpec(memory_...  1.31 us
    pallas_call x1, Pallas kernels, kernel_spectra(): pl.pallas_call(functools.partial(spectra_body, plan), out_shape=(jax.Shap...  1.19 us
    sub x1, other arithmetic, per_device(): logits = logits - step_size * first_hat / (jnp.sqrt(second_hat) + adam_eps)  0.69 us
  transfers between devices with their start and end apart: 8, of which 6 were waited for; matrix products, arithmetic and copies ran while one was open for 2% of the time, Pallas kernels for 18%

profile of v3, /device:TPU:9, one launch (start us, length us, event | category | flops | bytes accessed | tf_op | source)
XLA Modules:
  0.0 29.6 jit_solution(4742583763546119079)
XLA Ops:
  0.6 1.3 %fetch.1 = (bf16[48,256]{1,0:T(8,128)(2,1)S(1)}, f32[3,48,256]{2,1,0:T(8,128)S(1)}, bf16[48,512]{1,0:T(8,128)(2,1)S(1)}, f32[8,512]{1,0:T(8,128)S(1)}, f32[3,56,...) custom-call(f32[48,256]{1,0:T(8,128)} %logits_hbm.1, ...), custom_call_target="tpu_custom_call" | custom-call | tf_op jit(solution)/shard_map/fetch/pallas_call | solution.py:235
  2.0 0.7 %collective-permute-start.1 = (bf16[48,256]{1,0:T(8,128)(2,1)S(1)}, bf16[48,256]{1,0:T(8,128)(2,1)S(1)}, u32[]{:S(2)}, u32[]{:S(2)}) collective-permute-start(bf16[48,256]{1,0:T(8,128)(2,1)S(1)} %get-tuple-element.15), channel_id=1, source_target_pairs={{0,1},{1,0},{2,3},{3,2},{4,5},{5,4},{6,7},{7,6},{8,9},{9,8},{10,11... | collective-permute-start | bytes 73736 | tf_op jit(solution)/shard_map/ppermute | solution.py:470
  2.7 0.1 collective-permute-start
  2.9 0.7 %collective-permute-done.1 = bf16[48,256]{1,0:T(8,128)(2,1)S(1)} collective-permute-done((bf16[48,256]{1,0:T(8,128)(2,1)S(1)}, bf16[48,256]{1,0:T(8,128)(2,1)S(1)}, u32[]{:S(2)}, u32[]{:S(2)}) %collective-permute-start.1) | collective-permute-done | bytes 24608 | tf_op jit(solution)/shard_map/ppermute | solution.py:470
  3.6 1.2 %collective-permute-start.2 = (bf16[52,512]{1,0:T(8,128)(2,1)S(1)}, bf16[52,512]{1,0:T(8,128)(2,1)S(1)}, u32[]{:S(2)}, u32[]{:S(2)}) collective-permute-start(bf16[52,512]{1,0:T(8,128)(2,1)S(1)} %fusion.17), channel_id=1, source_target_pairs={{0,2},{2,4},{4,6},{6,8},{8,10},{10,12},{12,14},{14,15},{3,1},{5,3}... | collective-permute-start | bytes 159752 | tf_op jit(solution)/shard_map/ppermute | solution.py:479
  4.8 1.9 %collective-permute-done.2 = bf16[52,512]{1,0:T(8,128)(2,1)S(1)} collective-permute-done((bf16[52,512]{1,0:T(8,128)(2,1)S(1)}, bf16[52,512]{1,0:T(8,128)(2,1)S(1)}, u32[]{:S(2)}, u32[]{:S(2)}) %collective-permute-start.2) | collective-permute-done | bytes 53280 | tf_op jit(solution)/shard_map/ppermute | solution.py:479
  6.7 2.4 %collective-permute-start.3 = (bf16[52,512]{1,0:T(8,128)(2,1)S(1)}, bf16[52,512]{1,0:T(8,128)(2,1)S(1)}, u32[]{:S(2)}, u32[]{:S(2)}) collective-permute-start(bf16[52,512]{1,0:T(8,128)(2,1)S(1)} %collective-permute-done.2), channel_id=1, source_target_pairs={{0,1},{1,0},{2,3},{3,2},{4,5},{5,4},{6,7},{7,6},{8,9},{9,8},{10,11... | collective-permute-start | bytes 159752 | tf_op jit(solution)/shard_map/ppermute | solution.py:470
  9.2 0.1 pad.20.clone
  9.9 1.2 %spectra.1 = (f32[16,256,128]{2,1,0:T(8,128)S(1)}, f32[16,8,256]{2,1,0:T(8,128)S(1)}) custom-call(f32[8,8,256]{2,1,0:T(8,128)S(1)} %get-tuple-element.18.root_ref, f32[8,35,2,35]{3,2,1,0:T(2,128)S(1)} %get-tuple-element.19.kern_ref, bf16[352,256]{1,0:T(8,128)(2,1)S(1)} %get-tuple-element.20.table_ref), custom_call_target="tpu_custom_call" | custom-call | tf_op jit(solution)/shard_map/spectra/pallas_call | solution.py:281
  11.1 0.1 fusion.3
  11.3 0.1 maximum_maximum_fusion.2.target_ref
  11.4 0.1 maximum_maximum_fusion.mask_ref
  11.5 4.2 %gradient.2 = f32[48,512]{1,0:T(8,128)S(1)} custom-call(f32[8,128]{1,0:T(8,128)S(1)} %broadcast_in_dim.52.dose_ref, bf16[128,512]{1,0:T(8,128)(2,1)S(1)} %maximum_maximum_fusion.mask_ref, bf16[88,512]{1,0:T(8,128)(2,1)S(1)} %maximum_maximum_fusion.2.target_ref, f32[8,512]{1,0:T(8,128)S(1)} %add_divide_fusion.1.weight_ref, ...), custom_call_target="tpu_custom_call" | custom-call | tf_op jit(solution)/shard_map/gradient/pallas_call | solution.py:451
  15.9 1.2 %collective-permute-done.4 = bf16[48,512]{1,0:T(8,128)(2,1)S(1)} collective-permute-done((bf16[48,512]{1,0:T(8,128)(2,1)S(1)}, bf16[48,512]{1,0:T(8,128)(2,1)S(1)}, u32[]{:S(2)}, u32[]{:S(2)}) %collective-permute-start.4) | collective-permute-done | bytes 49184 | tf_op jit(solution)/shard_map/ppermute | solution.py:470
  17.1 0.1 add_convert_fusion
  17.3 0.9 %collective-permute-start.5 = (bf16[34,512]{1,0:T(8,128)(2,1)S(1)}, bf16[34,512]{1,0:T(8,128)(2,1)S(1)}, u32[]{:S(2)}, u32[]{:S(2)}) collective-permute-start(bf16[34,512]{1,0:T(8,128)(2,1)S(1)} %fusion.27), channel_id=1, source_target_pairs={{0,2},{2,4},{4,6},{6,8},{8,10},{10,12},{12,14},{14,15},{3,1},{5,3}... | collective-permute-start | bytes 104456 | tf_op jit(solution)/shard_map/ppermute | solution.py:479
  18.1 2.0 %collective-permute-done.5 = bf16[34,512]{1,0:T(8,128)(2,1)S(1)} collective-permute-done((bf16[34,512]{1,0:T(8,128)(2,1)S(1)}, bf16[34,512]{1,0:T(8,128)(2,1)S(1)}, u32[]{:S(2)}, u32[]{:S(2)}) %collective-permute-start.5) | collective-permute-done | bytes 34848 | tf_op jit(solution)/shard_map/ppermute | solution.py:479
  20.2 2.2 %collective-permute-start.6 = (bf16[34,512]{1,0:T(8,128)(2,1)S(1)}, bf16[34,512]{1,0:T(8,128)(2,1)S(1)}, u32[]{:S(2)}, u32[]{:S(2)}) collective-permute-start(bf16[34,512]{1,0:T(8,128)(2,1)S(1)} %collective-permute-done.5), channel_id=1, source_target_pairs={{0,1},{1,0},{2,3},{3,2},{4,5},{5,4},{6,7},{7,6},{8,9},{9,8},{10,11... | collective-permute-start | bytes 104456 | tf_op jit(solution)/shard_map/ppermute | solution.py:470
  22.4 0.9 %collective-permute-done.6 = bf16[34,512]{1,0:T(8,128)(2,1)S(1)} collective-permute-done((bf16[34,512]{1,0:T(8,128)(2,1)S(1)}, bf16[34,512]{1,0:T(8,128)(2,1)S(1)}, u32[]{:S(2)}, u32[]{:S(2)}) %collective-permute-start.6) | collective-permute-done | bytes 34848 | tf_op jit(solution)/shard_map/ppermute | solution.py:470
  23.3 0.1 maximum_maximum_fusion.1.mask_ref
  23.4 4.2 %gradient.3 = f32[48,512]{1,0:T(8,128)S(1)} custom-call(f32[8,128]{1,0:T(8,128)S(1)} %broadcast_in_dim.52.dose_ref, bf16[128,512]{1,0:T(8,128)(2,1)S(1)} %maximum_maximum_fusion.1.mask_ref, bf16[88,512]{1,0:T(8,128)(2,1)S(1)} %maximum_maximum_fusion.2.target_ref, f32[8,512]{1,0:T(8,128)S(1)} %add_divide_fusion.1.weight_ref, ...), custom_call_target="tpu_custom_call" | custom-call | tf_op jit(solution)/shard_map/gradient/pallas_call | solution.py:451
  27.6 0.4 %collective-permute-start.7 = (bf16[48,256]{1,0:T(8,128)(2,1)S(1)}, bf16[48,256]{1,0:T(8,128)(2,1)S(1)}, u32[]{:S(2)}, u32[]{:S(2)}) collective-permute-start(bf16[48,256]{1,0:T(8,128)(2,1)S(1)} %select_convert_fusion), channel_id=1, source_target_pairs={{0,1},{1,0},{2,3},{3,2},{4,5},{5,4},{6,7},{7,6},{8,9},{9,8},{10,11... | collective-permute-start | bytes 73736 | tf_op jit(solution)/shard_map/ppermute | solution.py:470
  28.0 0.8 %collective-permute-done.7 = bf16[48,256]{1,0:T(8,128)(2,1)S(1)} collective-permute-done((bf16[48,256]{1,0:T(8,128)(2,1)S(1)}, bf16[48,256]{1,0:T(8,128)(2,1)S(1)}, u32[]{:S(2)}, u32[]{:S(2)}) %collective-permute-start.7) | collective-permute-done | bytes 24608 | tf_op jit(solution)/shard_map/ppermute | solution.py:470
  28.9 0.7 %fusion.24 = (f32[48,256]{1,0:T(8,128)}, f32[48,256]{1,0:T(8,128)}, f32[48,256]{1,0:T(8,128)}) fusion(f32[48,512]{1,0:T(8,128)S(1)} %get-tuple-element.28, pred[3,56,512]{2,1,0:T(8,128)(4,1)S(1)} %broadcast_compare_fusion, f32[48,512]{1,0:T(8,128)S(1)} %get-tuple-element.29, f32[48,512]{1,0:T(8,128)S(1)} %get-tuple-element.30, ...), kind=kLoop, calls=%fused_computation.54 | loop fusion | flops 270336 | bytes 675840 | tf_op jit(solution)/shard_map/sub | solution.py:573
  (29 shorter events, 0.5 us)
Async XLA Ops:
  0.6 10.9 %copy-start = (bf16[2848,256]{1,0:T(8,128)(2,1)S(1)}, bf16[2848,256]{1,0:T(8,128)(2,1)}, u32[]{:S(2)}) copy-start(bf16[2848,256]{1,0:T(8,128)(2,1)} %constant.12.clone.table_ref) | copy-start | bytes 4374532
  2.0 1.6 %collective-permute-start.1 = (bf16[48,256]{1,0:T(8,128)(2,1)S(1)}, bf16[48,256]{1,0:T(8,128)(2,1)S(1)}, u32[]{:S(2)}, u32[]{:S(2)}) collective-permute-start(bf16[48,256]{1,0:T(8,128)(2,1)S(1)} %get-tuple-element.15), channel_id=1, source_target_pairs={{0,1},{1,0},{2,3},{3,2},{4,5},{5,4},{6,7},{7,6},{8,9},{9,8},{10,11... | collective-permute-start | bytes 73736 | tf_op jit(solution)/shard_map/ppermute | solution.py:470
  2.7 13.2 %collective-permute-start = (f32[3,48,256]{2,1,0:T(8,128)S(1)}, f32[3,48,256]{2,1,0:T(8,128)S(1)}, u32[]{:S(2)}, u32[]{:S(2)}) collective-permute-start(f32[3,48,256]{2,1,0:T(8,128)S(1)} %get-tuple-element.14), channel_id=1, source_target_pairs={{0,1},{1,0},{2,3},{3,2},{4,5},{5,4},{6,7},{7,6},{8,9},{9,8},{10,11... | collective-permute-start | bytes 442376 | tf_op jit(solution)/shard_map/ppermute | solution.py:470
  3.6 3.1 %collective-permute-start.2 = (bf16[52,512]{1,0:T(8,128)(2,1)S(1)}, bf16[52,512]{1,0:T(8,128)(2,1)S(1)}, u32[]{:S(2)}, u32[]{:S(2)}) collective-permute-start(bf16[52,512]{1,0:T(8,128)(2,1)S(1)} %fusion.17), channel_id=1, source_target_pairs={{0,2},{2,4},{4,6},{6,8},{8,10},{10,12},{12,14},{14,15},{3,1},{5,3}... | collective-permute-start | bytes 159752 | tf_op jit(solution)/shard_map/ppermute | solution.py:479
  6.7 4.4 %collective-permute-start.3 = (bf16[52,512]{1,0:T(8,128)(2,1)S(1)}, bf16[52,512]{1,0:T(8,128)(2,1)S(1)}, u32[]{:S(2)}, u32[]{:S(2)}) collective-permute-start(bf16[52,512]{1,0:T(8,128)(2,1)S(1)} %collective-permute-done.2), channel_id=1, source_target_pairs={{0,1},{1,0},{2,3},{3,2},{4,5},{5,4},{6,7},{7,6},{8,9},{9,8},{10,11... | collective-permute-start | bytes 159752 | tf_op jit(solution)/shard_map/ppermute | solution.py:470
  15.8 1.3 %collective-permute-start.4 = (bf16[48,512]{1,0:T(8,128)(2,1)S(1)}, bf16[48,512]{1,0:T(8,128)(2,1)S(1)}, u32[]{:S(2)}, u32[]{:S(2)}) collective-permute-start(bf16[48,512]{1,0:T(8,128)(2,1)S(1)} %convert_element_type.40), channel_id=1, source_target_pairs={{0,1},{1,0},{2,3},{3,2},{4,5},{5,4},{6,7},{7,6},{8,9},{9,8},{10,11... | collective-permute-start | bytes 147464 | tf_op jit(solution)/shard_map/ppermute | solution.py:470
  17.3 2.9 %collective-permute-start.5 = (bf16[34,512]{1,0:T(8,128)(2,1)S(1)}, bf16[34,512]{1,0:T(8,128)(2,1)S(1)}, u32[]{:S(2)}, u32[]{:S(2)}) collective-permute-start(bf16[34,512]{1,0:T(8,128)(2,1)S(1)} %fusion.27), channel_id=1, source_target_pairs={{0,2},{2,4},{4,6},{6,8},{8,10},{10,12},{12,14},{14,15},{3,1},{5,3}... | collective-permute-start | bytes 104456 | tf_op jit(solution)/shard_map/ppermute | solution.py:479
  20.2 3.1 %collective-permute-start.6 = (bf16[34,512]{1,0:T(8,128)(2,1)S(1)}, bf16[34,512]{1,0:T(8,128)(2,1)S(1)}, u32[]{:S(2)}, u32[]{:S(2)}) collective-permute-start(bf16[34,512]{1,0:T(8,128)(2,1)S(1)} %collective-permute-done.5), channel_id=1, source_target_pairs={{0,1},{1,0},{2,3},{3,2},{4,5},{5,4},{6,7},{7,6},{8,9},{9,8},{10,11... | collective-permute-start | bytes 104456 | tf_op jit(solution)/shard_map/ppermute | solution.py:470
  27.6 1.3 %collective-permute-start.7 = (bf16[48,256]{1,0:T(8,128)(2,1)S(1)}, bf16[48,256]{1,0:T(8,128)(2,1)S(1)}, u32[]{:S(2)}, u32[]{:S(2)}) collective-permute-start(bf16[48,256]{1,0:T(8,128)(2,1)S(1)} %select_convert_fusion), channel_id=1, source_target_pairs={{0,1},{1,0},{2,3},{3,2},{4,5},{5,4},{6,7},{7,6},{8,9},{9,8},{10,11... | collective-permute-start | bytes 73736 | tf_op jit(solution)/shard_map/ppermute | solution.py:470

commit v4 on v3

--- a/solution.py
+++ b/solution.py
@@ -169,16 +169,12 @@
     second_hbm,
     target_hbm,
     counts_hbm,
-    taps_hbm,
-    tables_hbm,
     socs_hbm,
     mask_ref,
     state_ref,
     target_ref,
     counts_ref,
     flags_ref,
-    taps_ref,
-    tables_ref,
     roots_ref,
     counts_smem,
     socs_smem,
@@ -190,8 +186,6 @@
         (target_hbm, target_ref),
         (first_hbm, state_ref.at[1]),
         (second_hbm, state_ref.at[2]),
-        (taps_hbm, taps_ref),
-        (tables_hbm, tables_ref),
         (socs_hbm, socs_smem),
     )
     copies = [pltpu.make_async_copy(a, b, sems.at[i]) for i, (a, b) in enumerate(pairs)]
@@ -215,12 +209,8 @@
         counts_ref[:, tile * wide : (tile + 1) * wide] = jnp.full((8, wide), value, F32)
 
 
-def fetch(
-    flag_rows, mask_logits, adam_first, adam_second, target, tile_counts, taps, tables, socs_weight
-):
-    args = (
-        mask_logits, adam_first, adam_second, target, tile_counts, taps, tables, socs_weight
-    )
+def fetch(flag_rows, mask_logits, adam_first, adam_second, target, tile_counts, socs_weight):
+    args = (mask_logits, adam_first, adam_second, target, tile_counts, socs_weight)
     shape = mask_logits.shape
     outs = (
         jax.ShapeDtypeStruct(shape, BF),
@@ -228,8 +218,6 @@
         jax.ShapeDtypeStruct(target.shape, BF),
         jax.ShapeDtypeStruct((8, target.shape[1]), F32),
         jax.ShapeDtypeStruct((3, flag_rows, target.shape[1]), F32),
-        jax.ShapeDtypeStruct(taps.shape, F32),
-        jax.ShapeDtypeStruct(tables.shape, BF),
         jax.ShapeDtypeStruct((socs_weight.shape[1], 8, COL_LEN), F32),
     )
     return pl.pallas_call(
@@ -247,7 +235,17 @@
     )(*(pltpu.with_memory_space_constraint(value, pltpu.HBM) for value in args))
 
 
-def spectra_body(plan, root_ref, kern_ref, table_ref, out_ref, level_ref):
+def spectra_body(
+    plan, root_ref, kern_hbm, table_hbm, out_ref, level_ref, kern_ref, table_ref, sems
+):
+    copies = [
+        pltpu.make_async_copy(kern_hbm, kern_ref, sems.at[0]),
+        pltpu.make_async_copy(table_hbm, table_ref, sems.at[1]),
+    ]
+    for copy in copies:
+        copy.start()
+    for copy in copies:
+        copy.wait()
     count = out_ref.shape[0]
     pad = plan.taps_pad - plan.taps
     stack, sums = [], []
@@ -275,7 +273,8 @@
         out_ref[k + 1] = spec[:, HALF_SPEC:] * root
 
 
-def kernel_spectra(plan, taps, tables, roots):
+def kernel_spectra(plan, kernels, roots):
+    taps, tables = kernels[0].transpose(0, 2, 1, 3), jnp.asarray(plan.tap_packed)
     count = 2 * taps.shape[0]
     vmem = pl.BlockSpec(memory_space=pltpu.VMEM)
     return pl.pallas_call(
@@ -284,11 +283,16 @@
             jax.ShapeDtypeStruct((count, 2 * plan.row_len, HALF_SPEC), F32),
             jax.ShapeDtypeStruct((count, 8, COL_LEN), F32),
         ),
-        in_specs=[vmem] * 3,
+        in_specs=[vmem] + [pl.BlockSpec(memory_space=pltpu.HBM)] * 2,
         out_specs=(vmem, vmem),
+        scratch_shapes=[
+            pltpu.VMEM(taps.shape, F32),
+            pltpu.VMEM(tables.shape, BF),
+            pltpu.SemaphoreType.DMA((2,)),
+        ],
         compiler_params=pltpu.CompilerParams(vmem_limit_bytes=4 * 1024 * 1024),
         name="spectra",
-    )(roots, taps, tables)
+    )(roots, *(pltpu.with_memory_space_constraint(value, pltpu.HBM) for value in (taps, tables)))
 
 
 def gradient_body(
@@ -325,8 +329,6 @@
             a = a + (edges[2:3] + edges[3:4])
         along.append(jnp.concatenate([a[:, :g], a[:, g:]], axis=0).astype(BF))
     s_ref[...] = dot(plan.table(table_ref, "row_fwd"), jnp.concatenate(along, axis=1))
-    light_ref[...] = jnp.zeros_like(light_ref)
-    acc_ref[...] = jnp.zeros_like(acc_ref)
     chunks = [(at, at + CHUNK, at + 2 * CHUNK) for at in range(0, 2 * rows, 2 * CHUNK)]
 
     groups = count // GROUP
@@ -350,12 +352,12 @@
             for part in range(GROUP):
                 lane = slice(part * g, part * g + g)
                 stack.append(jnp.concatenate([passed[t][:fr, lane], passed[t][fr:, lane]], axis=1))
-        hold_ref[group % 2] = jnp.concatenate(stack, axis=0).astype(BF)
+        hold_ref[group] = jnp.concatenate(stack, axis=0).astype(BF)
 
     def image(group):
-        field = dot(hold_ref[group % 2], plan.table(table_ref, "col_inv"))
+        field = dot(hold_ref[group], plan.table(table_ref, "col_inv"))
         for t in range(tiles):
-            total = light_ref[t]
+            total = light_ref[t] if group else 0.0
             for part in range(GROUP):
                 at = (GROUP * t + part) * fr
                 one = field[at : at + fr] + level_ref[GROUP * group + part, :1]
@@ -363,14 +365,11 @@
                 total = total + one * one
             light_ref[t] = total
 
-    def forward(group, carry):
+    multiply(0)
+    for group in range(groups):
         image(group)
-        multiply(group + 1)
-        return carry
-
-    multiply(0)
-    lax.fori_loop(0, groups - 1, forward, 0, unroll=True)
-    image(groups - 1)
+        if group + 1 < groups:
+            multiply(group + 1)
 
     dose = dose_ref[:1, :1]
     row = lax.broadcasted_iota(jnp.int32, (fr, COL_LEN), 0)
@@ -408,7 +407,7 @@
             lane = slice(t * g, t * g + g)
             d_prod = dot(plan.table(table_ref, "row_inv_adj"), back_ref[group % 4, t])
             for a, b, c in chunks:
-                sum_re, sum_im = acc_ref[a:b, lane], acc_ref[b:c, lane]
+                sum_re, sum_im = (acc_ref[a:b, lane], acc_ref[b:c, lane]) if group else (0.0, 0.0)
                 for part in range(GROUP):
                     k = GROUP * group + part
                     k_re, k_im = spec_ref[k, a:b], spec_ref[k, b:c]
@@ -419,12 +418,13 @@
                 acc_ref[a:b, lane] = sum_re
                 acc_ref[b:c, lane] = sum_im
 
-    for group in range(1):
-        image_back(group, range(tiles))
+    for t in range(tiles):
+        image_back(0, (t,))
     for group in range(groups):
-        if group + 1 < groups:
-            image_back(group + 1, range(tiles))
-        multiply_back(group, range(tiles))
+        for t in range(tiles):
+            multiply_back(group, (t,))
+            if group + 1 < groups:
+                image_back(group + 1, (t,))
 
     d_along = dot(plan.table(table_ref, "row_adj"), acc_ref[...].astype(BF))
     parts = []
@@ -458,7 +458,7 @@
             pltpu.VMEM((count // GROUP, GROUP * plan.col_tiles * plan.field_pad, COL_LEN), F32),
             pltpu.VMEM(image, F32),
             pltpu.VMEM(spectrum, F32),
-            pltpu.VMEM((2, GROUP * plan.col_tiles * plan.field_pad, COL_LEN), BF),
+            pltpu.VMEM((count // GROUP, GROUP * plan.col_tiles * plan.field_pad, COL_LEN), BF),
             pltpu.VMEM((4, plan.col_tiles, 2 * plan.field_pad, GROUP * HALF_SPEC), BF),
         ],
         compiler_params=pltpu.CompilerParams(vmem_limit_bytes=12 * 1024 * 1024),
@@ -509,15 +509,13 @@
 
     tables = jnp.asarray(plan.packed)
 
-    mask_half, state, target, counts, facts, taps, tap_tables, roots = fetch(
+    mask_half, state, target, counts, facts, roots = fetch(
         up_to(max(strip_rows, halo + reach + 1), 8),
         mask_logits,
         adam_first,
         adam_second,
         target,
         tile_counts,
-        kernels[0].transpose(0, 2, 1, 3),
-        jnp.asarray(plan.tap_packed),
         socs_weight,
     )
     flags = facts > 0.5
@@ -532,7 +530,7 @@
         jnp.concatenate([mask_bf[-halo:], target[-reach:], counts_bf], axis=0),
         jnp.where(jnp.arange(halo + reach + 1)[:, None] < halo, -MIDDLE, 0.0).astype(BF),
     )
-    spec = kernel_spectra(plan, taps, tap_tables, roots)
+    spec = kernel_spectra(plan, kernels, roots)
     target_ext = extended(
         above[halo : halo + reach], target, below[halo : halo + reach], plan.field_pad
     )

time: 29.7 us -> 30.7 us (1.034)
  Pallas kernels: 11 us -> 11.9 us
    pallas_call x1, Pallas kernels: 1.19 us -> 2.21 us  [kernel_spectra(): pl.pallas_call(functools.partial(spectra_body, plan), out_shape=(jax.Shap...]
  transfers between devices with their start and end apart: 8 -> 8, of which waited for: 6 -> 6; matrix products, arithmetic and copies ran while one was open for 2% -> 2% of each run, Pallas kernels for 18% -> 21%
where the time goes in v4:
time: 30.7 us; the launch traced here: 30.5 us
  Pallas kernels  11.9 us (39%)
  starting transfers between devices  7.93 us (26%)
  waiting for transfers between devices  7.55 us (25%)
  between operations  1.49 us (5%)
  other arithmetic  1.43 us (5%)
    pallas_call x2, Pallas kernels, strip_gradient(): pl.pallas_call(functools.partial(gradient_body, plan), out_shape=jax.Shap...  8.66 us
    ppermute x6, starting transfers between devices, other_corner(): return lax.ppermute(value, 'corner', [(0, 1), (1, 0)])  5.91 us
    ppermute x2, waiting for transfers between devices, neighbours(): got = lax.ppermute(message, ('tile', 'corner'), cycle)  3.97 us
    ppermute x6, waiting for transfers between devices, other_corner(): return lax.ppermute(value, 'corner', [(0, 1), (1, 0)])  3.58 us
    pallas_call x1, Pallas kernels, kernel_spectra(): pl.pallas_call(functools.partial(spectra_body, plan), out_shape=(jax.Shap...  2.21 us
    ppermute x2, starting transfers between devices, neighbours(): got = lax.ppermute(message, ('tile', 'corner'), cycle)  2.03 us
    pallas_call x1, Pallas kernels, fetch(): pl.pallas_call(fetch_body, out_shape=outs, in_specs=[pl.BlockSpec(memory_...  1.06 us
    sub x1, other arithmetic, per_device(): logits = logits - step_size * first_hat / (jnp.sqrt(second_hat) + adam_eps)  0.69 us
  transfers between devices with their start and end apart: 8, of which 6 were waited for; matrix products, arithmetic and copies ran while one was open for 2% of the time, Pallas kernels for 21%

profile of v4, /device:TPU:9, one launch (start us, length us, event | category | flops | bytes accessed | tf_op | source)
XLA Modules:
  0.0 30.5 jit_solution(8171801414063560998)
XLA Ops:
  0.6 1.1 %fetch.1 = (bf16[48,256]{1,0:T(8,128)(2,1)S(1)}, f32[3,48,256]{2,1,0:T(8,128)S(1)}, bf16[48,512]{1,0:T(8,128)(2,1)S(1)}, f32[8,512]{1,0:T(8,128)S(1)}, f32[3,56,...) custom-call(f32[48,256]{1,0:T(8,128)} %logits_hbm.1, f32[48,256]{1,0:T(8,128)} %first_hbm.1, f32[48,256]{1,0:T(8,128)} %second_hbm.1, ...), custom_call_target="tpu_custom_call" | custom-call | tf_op jit(solution)/shard_map/fetch/pallas_call | solution.py:223
  1.7 0.7 %collective-permute-start.1 = (bf16[48,256]{1,0:T(8,128)(2,1)S(1)}, bf16[48,256]{1,0:T(8,128)(2,1)S(1)}, u32[]{:S(2)}, u32[]{:S(2)}) collective-permute-start(bf16[48,256]{1,0:T(8,128)(2,1)S(1)} %get-tuple-element.13), channel_id=1, source_target_pairs={{0,1},{1,0},{2,3},{3,2},{4,5},{5,4},{6,7},{7,6},{8,9},{9,8},{10,11... | collective-permute-start | bytes 73736 | tf_op jit(solution)/shard_map/ppermute | solution.py:470
  2.5 0.1 collective-permute-start
  2.6 0.7 %collective-permute-done.1 = bf16[48,256]{1,0:T(8,128)(2,1)S(1)} collective-permute-done((bf16[48,256]{1,0:T(8,128)(2,1)S(1)}, bf16[48,256]{1,0:T(8,128)(2,1)S(1)}, u32[]{:S(2)}, u32[]{:S(2)}) %collective-permute-start.1) | collective-permute-done | bytes 24608 | tf_op jit(solution)/shard_map/ppermute | solution.py:470
  3.4 1.2 %collective-permute-start.2 = (bf16[52,512]{1,0:T(8,128)(2,1)S(1)}, bf16[52,512]{1,0:T(8,128)(2,1)S(1)}, u32[]{:S(2)}, u32[]{:S(2)}) collective-permute-start(bf16[52,512]{1,0:T(8,128)(2,1)S(1)} %fusion.17), channel_id=1, source_target_pairs={{0,2},{2,4},{4,6},{6,8},{8,10},{10,12},{12,14},{14,15},{3,1},{5,3}... | collective-permute-start | bytes 159752 | tf_op jit(solution)/shard_map/ppermute | solution.py:479
  4.5 1.9 %collective-permute-done.2 = bf16[52,512]{1,0:T(8,128)(2,1)S(1)} collective-permute-done((bf16[52,512]{1,0:T(8,128)(2,1)S(1)}, bf16[52,512]{1,0:T(8,128)(2,1)S(1)}, u32[]{:S(2)}, u32[]{:S(2)}) %collective-permute-start.2) | collective-permute-done | bytes 53280 | tf_op jit(solution)/shard_map/ppermute | solution.py:479
  6.5 2.4 %collective-permute-start.3 = (bf16[52,512]{1,0:T(8,128)(2,1)S(1)}, bf16[52,512]{1,0:T(8,128)(2,1)S(1)}, u32[]{:S(2)}, u32[]{:S(2)}) collective-permute-start(bf16[52,512]{1,0:T(8,128)(2,1)S(1)} %collective-permute-done.2), channel_id=1, source_target_pairs={{0,1},{1,0},{2,3},{3,2},{4,5},{5,4},{6,7},{7,6},{8,9},{9,8},{10,11... | collective-permute-start | bytes 159752 | tf_op jit(solution)/shard_map/ppermute | solution.py:470
  9.6 0.1 pad.20.clone
  9.7 2.2 %spectra.1 = (f32[16,256,128]{2,1,0:T(8,128)S(1)}, f32[16,8,256]{2,1,0:T(8,128)S(1)}) custom-call(f32[8,8,256]{2,1,0:T(8,128)S(1)} %get-tuple-element.16.root_ref, f32[8,35,2,35]{3,2,1,0:T(2,128)} %bitcast.80, bf16[352,256]{1,0:T(8,128)(2,1)} %constant.13.clone.table_hbm), custom_call_target="tpu_custom_call" | custom-call | tf_op jit(solution)/shard_map/spectra/pallas_call | solution.py:280
  11.9 0.1 fusion.3
  12.1 0.1 maximum_maximum_fusion.2.target_ref
  12.2 0.1 maximum_maximum_fusion.mask_ref
  12.3 4.3 %gradient.2 = f32[48,512]{1,0:T(8,128)S(1)} custom-call(f32[8,128]{1,0:T(8,128)S(1)} %broadcast_in_dim.52.dose_ref, bf16[128,512]{1,0:T(8,128)(2,1)S(1)} %maximum_maximum_fusion.mask_ref, bf16[88,512]{1,0:T(8,128)(2,1)S(1)} %maximum_maximum_fusion.2.target_ref, f32[8,512]{1,0:T(8,128)S(1)} %add_divide_fusion.1.weight_ref, ...), custom_call_target="tpu_custom_call" | custom-call | tf_op jit(solution)/shard_map/gradient/pallas_call | solution.py:451
  16.8 1.2 %collective-permute-done.4 = bf16[48,512]{1,0:T(8,128)(2,1)S(1)} collective-permute-done((bf16[48,512]{1,0:T(8,128)(2,1)S(1)}, bf16[48,512]{1,0:T(8,128)(2,1)S(1)}, u32[]{:S(2)}, u32[]{:S(2)}) %collective-permute-start.4) | collective-permute-done | bytes 49184 | tf_op jit(solution)/shard_map/ppermute | solution.py:470
  18.0 0.1 add_convert_fusion
  18.1 0.9 %collective-permute-start.5 = (bf16[34,512]{1,0:T(8,128)(2,1)S(1)}, bf16[34,512]{1,0:T(8,128)(2,1)S(1)}, u32[]{:S(2)}, u32[]{:S(2)}) collective-permute-start(bf16[34,512]{1,0:T(8,128)(2,1)S(1)} %fusion.27), channel_id=1, source_target_pairs={{0,2},{2,4},{4,6},{6,8},{8,10},{10,12},{12,14},{14,15},{3,1},{5,3}... | collective-permute-start | bytes 104456 | tf_op jit(solution)/shard_map/ppermute | solution.py:479
  19.0 2.0 %collective-permute-done.5 = bf16[34,512]{1,0:T(8,128)(2,1)S(1)} collective-permute-done((bf16[34,512]{1,0:T(8,128)(2,1)S(1)}, bf16[34,512]{1,0:T(8,128)(2,1)S(1)}, u32[]{:S(2)}, u32[]{:S(2)}) %collective-permute-start.5) | collective-permute-done | bytes 34848 | tf_op jit(solution)/shard_map/ppermute | solution.py:479
  21.0 2.2 %collective-permute-start.6 = (bf16[34,512]{1,0:T(8,128)(2,1)S(1)}, bf16[34,512]{1,0:T(8,128)(2,1)S(1)}, u32[]{:S(2)}, u32[]{:S(2)}) collective-permute-start(bf16[34,512]{1,0:T(8,128)(2,1)S(1)} %collective-permute-done.5), channel_id=1, source_target_pairs={{0,1},{1,0},{2,3},{3,2},{4,5},{5,4},{6,7},{7,6},{8,9},{9,8},{10,11... | collective-permute-start | bytes 104456 | tf_op jit(solution)/shard_map/ppermute | solution.py:470
  23.3 0.9 %collective-permute-done.6 = bf16[34,512]{1,0:T(8,128)(2,1)S(1)} collective-permute-done((bf16[34,512]{1,0:T(8,128)(2,1)S(1)}, bf16[34,512]{1,0:T(8,128)(2,1)S(1)}, u32[]{:S(2)}, u32[]{:S(2)}) %collective-permute-start.6) | collective-permute-done | bytes 34848 | tf_op jit(solution)/shard_map/ppermute | solution.py:470
  24.1 0.1 maximum_maximum_fusion.1.mask_ref
  24.2 4.3 %gradient.3 = f32[48,512]{1,0:T(8,128)S(1)} custom-call(f32[8,128]{1,0:T(8,128)S(1)} %broadcast_in_dim.52.dose_ref, bf16[128,512]{1,0:T(8,128)(2,1)S(1)} %maximum_maximum_fusion.1.mask_ref, bf16[88,512]{1,0:T(8,128)(2,1)S(1)} %maximum_maximum_fusion.2.target_ref, f32[8,512]{1,0:T(8,128)S(1)} %add_divide_fusion.1.weight_ref, ...), custom_call_target="tpu_custom_call" | custom-call | tf_op jit(solution)/shard_map/gradient/pallas_call | solution.py:451
  28.6 0.4 %collective-permute-start.7 = (bf16[48,256]{1,0:T(8,128)(2,1)S(1)}, bf16[48,256]{1,0:T(8,128)(2,1)S(1)}, u32[]{:S(2)}, u32[]{:S(2)}) collective-permute-start(bf16[48,256]{1,0:T(8,128)(2,1)S(1)} %select_convert_fusion), channel_id=1, source_target_pairs={{0,1},{1,0},{2,3},{3,2},{4,5},{5,4},{6,7},{7,6},{8,9},{9,8},{10,11... | collective-permute-start | bytes 73736 | tf_op jit(solution)/shard_map/ppermute | solution.py:470
  29.0 0.8 %collective-permute-done.7 = bf16[48,256]{1,0:T(8,128)(2,1)S(1)} collective-permute-done((bf16[48,256]{1,0:T(8,128)(2,1)S(1)}, bf16[48,256]{1,0:T(8,128)(2,1)S(1)}, u32[]{:S(2)}, u32[]{:S(2)}) %collective-permute-start.7) | collective-permute-done | bytes 24608 | tf_op jit(solution)/shard_map/ppermute | solution.py:470
  29.9 0.7 %fusion.24 = (f32[48,256]{1,0:T(8,128)}, f32[48,256]{1,0:T(8,128)}, f32[48,256]{1,0:T(8,128)}) fusion(f32[48,512]{1,0:T(8,128)S(1)} %get-tuple-element.24, pred[3,56,512]{2,1,0:T(8,128)(4,1)S(1)} %broadcast_compare_fusion, f32[48,512]{1,0:T(8,128)S(1)} %get-tuple-element.25, f32[48,512]{1,0:T(8,128)S(1)} %get-tuple-element.26, ...), kind=kLoop, calls=%fused_computation.54 | loop fusion | flops 270336 | bytes 675840 | tf_op jit(solution)/shard_map/sub | solution.py:571
  (29 shorter events, 0.5 us)
Async XLA Ops:
  0.6 11.7 %copy-start = (bf16[2848,256]{1,0:T(8,128)(2,1)S(1)}, bf16[2848,256]{1,0:T(8,128)(2,1)}, u32[]{:S(2)}) copy-start(bf16[2848,256]{1,0:T(8,128)(2,1)} %constant.12.clone.table_ref) | copy-start | bytes 4374532
  1.7 1.6 %collective-permute-start.1 = (bf16[48,256]{1,0:T(8,128)(2,1)S(1)}, bf16[48,256]{1,0:T(8,128)(2,1)S(1)}, u32[]{:S(2)}, u32[]{:S(2)}) collective-permute-start(bf16[48,256]{1,0:T(8,128)(2,1)S(1)} %get-tuple-element.13), channel_id=1, source_target_pairs={{0,1},{1,0},{2,3},{3,2},{4,5},{5,4},{6,7},{7,6},{8,9},{9,8},{10,11... | collective-permute-start | bytes 73736 | tf_op jit(solution)/shard_map/ppermute | solution.py:470
  2.5 14.3 %collective-permute-start = (f32[3,48,256]{2,1,0:T(8,128)S(1)}, f32[3,48,256]{2,1,0:T(8,128)S(1)}, u32[]{:S(2)}, u32[]{:S(2)}) collective-permute-start(f32[3,48,256]{2,1,0:T(8,128)S(1)} %get-tuple-element.12), channel_id=1, source_target_pairs={{0,1},{1,0},{2,3},{3,2},{4,5},{5,4},{6,7},{7,6},{8,9},{9,8},{10,11... | collective-permute-start | bytes 442376 | tf_op jit(solution)/shard_map/ppermute | solution.py:470
  3.4 3.1 %collective-permute-start.2 = (bf16[52,512]{1,0:T(8,128)(2,1)S(1)}, bf16[52,512]{1,0:T(8,128)(2,1)S(1)}, u32[]{:S(2)}, u32[]{:S(2)}) collective-permute-start(bf16[52,512]{1,0:T(8,128)(2,1)S(1)} %fusion.17), channel_id=1, source_target_pairs={{0,2},{2,4},{4,6},{6,8},{8,10},{10,12},{12,14},{14,15},{3,1},{5,3}... | collective-permute-start | bytes 159752 | tf_op jit(solution)/shard_map/ppermute | solution.py:479
  6.5 5.4 %collective-permute-start.3 = (bf16[52,512]{1,0:T(8,128)(2,1)S(1)}, bf16[52,512]{1,0:T(8,128)(2,1)S(1)}, u32[]{:S(2)}, u32[]{:S(2)}) collective-permute-start(bf16[52,512]{1,0:T(8,128)(2,1)S(1)} %collective-permute-done.2), channel_id=1, source_target_pairs={{0,1},{1,0},{2,3},{3,2},{4,5},{5,4},{6,7},{7,6},{8,9},{9,8},{10,11... | collective-permute-start | bytes 159752 | tf_op jit(solution)/shard_map/ppermute | solution.py:470
  16.7 1.3 %collective-permute-start.4 = (bf16[48,512]{1,0:T(8,128)(2,1)S(1)}, bf16[48,512]{1,0:T(8,128)(2,1)S(1)}, u32[]{:S(2)}, u32[]{:S(2)}) collective-permute-start(bf16[48,512]{1,0:T(8,128)(2,1)S(1)} %convert_element_type.40), channel_id=1, source_target_pairs={{0,1},{1,0},{2,3},{3,2},{4,5},{5,4},{6,7},{7,6},{8,9},{9,8},{10,11... | collective-permute-start | bytes 147464 | tf_op jit(solution)/shard_map/ppermute | solution.py:470
  18.1 2.9 %collective-permute-start.5 = (bf16[34,512]{1,0:T(8,128)(2,1)S(1)}, bf16[34,512]{1,0:T(8,128)(2,1)S(1)}, u32[]{:S(2)}, u32[]{:S(2)}) collective-permute-start(bf16[34,512]{1,0:T(8,128)(2,1)S(1)} %fusion.27), channel_id=1, source_target_pairs={{0,2},{2,4},{4,6},{6,8},{8,10},{10,12},{12,14},{14,15},{3,1},{5,3}... | collective-permute-start | bytes 104456 | tf_op jit(solution)/shard_map/ppermute | solution.py:479
  21.0 3.1 %collective-permute-start.6 = (bf16[34,512]{1,0:T(8,128)(2,1)S(1)}, bf16[34,512]{1,0:T(8,128)(2,1)S(1)}, u32[]{:S(2)}, u32[]{:S(2)}) collective-permute-start(bf16[34,512]{1,0:T(8,128)(2,1)S(1)} %collective-permute-done.5), channel_id=1, source_target_pairs={{0,1},{1,0},{2,3},{3,2},{4,5},{5,4},{6,7},{7,6},{8,9},{9,8},{10,11... | collective-permute-start | bytes 104456 | tf_op jit(solution)/shard_map/ppermute | solution.py:470
  28.6 1.3 %collective-permute-start.7 = (bf16[48,256]{1,0:T(8,128)(2,1)S(1)}, bf16[48,256]{1,0:T(8,128)(2,1)S(1)}, u32[]{:S(2)}, u32[]{:S(2)}) collective-permute-start(bf16[48,256]{1,0:T(8,128)(2,1)S(1)} %select_convert_fusion), channel_id=1, source_target_pairs={{0,1},{1,0},{2,3},{3,2},{4,5},{5,4},{6,7},{7,6},{8,9},{9,8},{10,11... | collective-permute-start | bytes 73736 | tf_op jit(solution)/shard_map/ppermute | solution.py:470
